TPU v7x, 32 devices: a whole 2x2x4 slice. The times are simulated.
32 devices in a mesh: grp: 4 (over x, core), rows: 8 (over z, y).
Axes of the slice: x: 2, y: 2, z: 4, core: 2. Of those that a mesh axis runs over, the one named last changes fastest.
Arguments:
- table_rows: bfloat16 [8, 2048, 768], P('rows', 'grp'), may hold values from -6 to 6
- cotangent: bfloat16 [8, 2048, 768], P('rows', 'grp'), may hold values from -6 to 6
- w_query: bfloat16 [768, 768], replicated, may hold values from -0.21875 to 0.21875
- w_key: bfloat16 [768, 768], replicated, may hold values from -0.21875 to 0.21875
- w_value: bfloat16 [768, 768], replicated, may hold values from -0.21875 to 0.21875
- w_out: bfloat16 [768, 768], replicated, may hold values from -1.75 to 1.75
- w_up: bfloat16 [768, 3072], replicated, may hold values from -0.21875 to 0.21875
- w_down: bfloat16 [3072, 768], replicated, may hold values from -0.109375 to 0.109375
- b_up: float32 [3072], replicated, may hold values from -3 to 3
- b_down: float32 [768], replicated, may hold values from -2 to 2
- g_one: float32 [768], replicated, may hold values from 0.5 to 1.5
- b_one: float32 [768], replicated, may hold values from -2 to 2
- g_two: float32 [768], replicated, may hold values from 0.5 to 1.5
- b_two: float32 [768], replicated, may hold values from -2 to 2
- ctx_count: int32 [8], P('rows'), may hold values from 1024 to 1536
- qry_count: int32 [8], P('rows'), may hold values from 256 to 512
- key_keep: int32 [8, 2048], P('rows'), may hold values from 0 to 1
Outputs:
- result: bfloat16 [8, 2048, 768], P('rows', 'grp')
- d_rows: bfloat16 [8, 2048, 768], P('rows', 'grp')
- d_w_query: float32 [768, 768], replicated
- d_w_key: float32 [768, 768], replicated
- d_w_value: float32 [768, 768], replicated
- d_w_out: float32 [768, 768], replicated
- d_w_up: float32 [768, 3072], replicated
- d_w_down: float32 [3072, 768], replicated
- d_b_up: float32 [3072], replicated
- d_b_down: float32 [768], replicated
- d_g_one: float32 [768], replicated
- d_b_one: float32 [768], replicated
- d_g_two: float32 [768], replicated
- d_b_two: float32 [768], replicated
All inputs are finite; a program needn't handle non-finite values.
Results may differ from a plain program's by a relative error of at most 0.013.
Values may be sent and summed in bfloat16 or wider, within the bound.
No kernel may reach another device: no remote copies, remote signals or barrier semaphores. Data moves between devices by JAX's collectives and lax.ppermute only.
A program may use at most 320 MiB of HBM per device.

v0:
```python
from functools import partial

import jax
import jax.numpy as jnp
from jax import lax
from jax.sharding import PartitionSpec as P

H = 12
DH = 64


epsilon = 1e-05


def layer_norm(values, gain_vec, shift_vec):
    row_mean = jnp.mean(values, axis=-1, keepdims=True)
    centred = values - row_mean
    spread = jnp.mean(centred * centred, axis=-1, keepdims=True)
    return centred * lax.rsqrt(spread + epsilon) * gain_vec + shift_vec


def gelu_tanh(values):
    return jax.nn.gelu(values, approximate=True)


def outer_sum(left_side, right_side):
    return lax.dot_general(
        left_side, right_side, (((0,), (0,)), ((), ())), preferred_element_type=jnp.float32
    )


def back_product(grad_in, weight):
    return lax.dot_general(
        grad_in, weight, (((1,), (1,)), ((), ())), preferred_element_type=jnp.float32
    )


def head_part(matrix, first_head, group_size):
    return matrix[:, first_head * DH : (first_head + group_size) * DH].reshape(
        matrix.shape[0], group_size, DH
    )


def masked_scores(q_part, k_part, key_ok):
    score_scale = DH ** (-0.5)
    scores = (
        jnp.einsum("qhd,khd->hqk", q_part, k_part, preferred_element_type=jnp.float32) * score_scale
    )
    return jnp.where(key_ok[None, None, :], scores, -1e30)


def attend_forward(inputs_one, group_size):
    queries, key_rows, value_rows, key_ok = inputs_one
    heads_here = queries.shape[1] // DH
    pieces, highest_all, totals_all = ([], [], [])
    for first_head in range(0, heads_here, group_size):
        q_part = head_part(queries, first_head, group_size)
        k_part = head_part(key_rows, first_head, group_size)
        v_part = head_part(value_rows, first_head, group_size)
        scores = masked_scores(q_part, k_part, key_ok)
        highest = jnp.max(scores, axis=-1, keepdims=True)
        exp_scores = jnp.exp(scores - highest)
        row_total = jnp.sum(exp_scores, axis=-1, keepdims=True)
        probs_low = (exp_scores / row_total).astype(jnp.bfloat16)
        mixed_part = jnp.einsum(
            "hqk,khd->qhd", probs_low, v_part, preferred_element_type=jnp.float32
        )
        pieces.append(mixed_part.reshape(queries.shape[0], group_size * DH))
        highest_all.append(highest)
        totals_all.append(row_total)
    mixed_out = jnp.concatenate(pieces, axis=1).astype(jnp.bfloat16)
    return (mixed_out, jnp.concatenate(highest_all, axis=0), jnp.concatenate(totals_all, axis=0))


def attend_backward(inputs_one, group_size):
    queries, key_rows, value_rows, key_ok, d_mixed, highest, row_total = inputs_one
    heads_here = queries.shape[1] // DH
    score_scale = DH ** (-0.5)
    q_grads, k_grads, v_grads = ([], [], [])
    for first_head in range(0, heads_here, group_size):
        q_part = head_part(queries, first_head, group_size)
        k_part = head_part(key_rows, first_head, group_size)
        v_part = head_part(value_rows, first_head, group_size)
        grad_part = head_part(d_mixed, first_head, group_size)
        high_part = highest[first_head : first_head + group_size]
        total_part = row_total[first_head : first_head + group_size]
        scores = masked_scores(q_part, k_part, key_ok)
        probs_full = jnp.exp(scores - high_part) / total_part
        probs_low = probs_full.astype(jnp.bfloat16)
        d_probs = jnp.einsum("qhd,khd->hqk", grad_part, v_part, preferred_element_type=jnp.float32)
        inner_sum = jnp.sum(probs_full * d_probs, axis=-1, keepdims=True)
        d_scores = (probs_full * (d_probs - inner_sum)).astype(jnp.bfloat16)
        q_grad = (
            jnp.einsum("hqk,khd->qhd", d_scores, k_part, preferred_element_type=jnp.float32)
            * score_scale
        )
        k_grad = (
            jnp.einsum("hqk,qhd->khd", d_scores, q_part, preferred_element_type=jnp.float32)
            * score_scale
        )
        v_grad = jnp.einsum(
            "hqk,qhd->khd", probs_low, grad_part, preferred_element_type=jnp.float32
        )
        q_grads.append(q_grad.reshape(queries.shape[0], group_size * DH))
        k_grads.append(k_grad.reshape(key_rows.shape[0], group_size * DH))
        v_grads.append(v_grad.reshape(key_rows.shape[0], group_size * DH))
    d_query = jnp.concatenate(q_grads, axis=1).astype(jnp.bfloat16)
    return (d_query, jnp.concatenate(k_grads, axis=1), jnp.concatenate(v_grads, axis=1))


def shards(
    table_rows,
    cotangent,
    w_query,
    w_key,
    w_value,
    w_out,
    w_up,
    w_down,
    b_up,
    b_down,
    g_one,
    b_one,
    g_two,
    b_two,
    ctx_count,
    qry_count,
    key_keep,
):
    tables, local_rows, model_width = table_rows.shape
    slot_count = key_keep.shape[1]
    position = lax.axis_index("grp") * local_rows + jnp.arange(local_rows, dtype=jnp.int32)
    row_ok = position[None, :] < (ctx_count + qry_count)[:, None]
    key_ok = (jnp.arange(slot_count, dtype=jnp.int32)[None, :] < ctx_count[:, None]) & (
        key_keep == 1
    )
    row_mask = row_ok.reshape(-1, 1)
    row_data = table_rows.astype(jnp.float32).reshape(-1, model_width)
    normed = layer_norm(row_data, g_one, b_one).astype(jnp.bfloat16)
    queries = (
        jnp.dot(normed, w_query, preferred_element_type=jnp.float32)
        .astype(jnp.bfloat16)
        .reshape(tables, local_rows, model_width)
    )
    key_rows = (
        jnp.dot(normed, w_key, preferred_element_type=jnp.float32)
        .astype(jnp.bfloat16)
        .reshape(tables, local_rows, model_width)
    )
    value_rows = (
        jnp.dot(normed, w_value, preferred_element_type=jnp.float32)
        .astype(jnp.bfloat16)
        .reshape(tables, local_rows, model_width)
    )
    all_keys, all_values = (
        lax.all_gather(key_rows, "grp", axis=1, tiled=True),
        lax.all_gather(value_rows, "grp", axis=1, tiled=True),
    )
    mixed_out, highest, row_total = lax.map(
        partial(attend_forward, group_size=min(4, H)), (queries, all_keys, all_values, key_ok)
    )
    mixed_flat = mixed_out.reshape(-1, model_width)
    first_sum = row_data + jnp.dot(mixed_flat, w_out, preferred_element_type=jnp.float32)
    normed_two = layer_norm(first_sum, g_two, b_two).astype(jnp.bfloat16)
    hidden = jnp.dot(normed_two, w_up, preferred_element_type=jnp.float32) + b_up
    active = gelu_tanh(hidden).astype(jnp.bfloat16)
    second_sum = first_sum + jnp.dot(active, w_down, preferred_element_type=jnp.float32) + b_down
    result = (
        jnp.where(row_mask, second_sum, 0.0)
        .astype(jnp.bfloat16)
        .reshape(tables, local_rows, model_width)
    )
    grad_out = jnp.where(row_mask, cotangent.astype(jnp.float32).reshape(-1, model_width), 0.0)
    grad_low = grad_out.astype(jnp.bfloat16)
    d_w_down = outer_sum(active, grad_low)
    d_b_down = jnp.sum(grad_out, axis=0)
    d_active = back_product(grad_low, w_down)
    gelu_pull = jax.vjp(gelu_tanh, hidden)[1]
    d_hidden = gelu_pull(d_active)[0].astype(jnp.bfloat16)
    d_b_up = jnp.sum(d_hidden, axis=0, dtype=jnp.float32)
    d_w_up = outer_sum(normed_two, d_hidden)
    d_normed_two = back_product(d_hidden, w_up)
    second_pull = jax.vjp(layer_norm, first_sum, g_two, b_two)[1]
    d_first_norm, d_g_two, d_b_two = second_pull(d_normed_two)
    d_first = grad_out + d_first_norm
    d_first_low = d_first.astype(jnp.bfloat16)
    d_w_out = outer_sum(mixed_flat, d_first_low)
    d_mixed = (
        back_product(d_first_low, w_out)
        .astype(jnp.bfloat16)
        .reshape(tables, local_rows, model_width)
    )
    back_keys, back_values = (
        lax.all_gather(key_rows, "grp", axis=1, tiled=True),
        lax.all_gather(value_rows, "grp", axis=1, tiled=True),
    )
    d_query, d_keys_all, d_values_all = lax.map(
        partial(attend_backward, group_size=min(4, H)),
        (queries, back_keys, back_values, key_ok, d_mixed, highest, row_total),
    )
    d_keys, d_values = (
        lax.psum_scatter(
            d_keys_all.astype(jnp.bfloat16), "grp", scatter_dimension=1, tiled=True
        ).astype(jnp.float32),
        lax.psum_scatter(
            d_values_all.astype(jnp.bfloat16), "grp", scatter_dimension=1, tiled=True
        ).astype(jnp.float32),
    )
    d_query_low = d_query.reshape(-1, model_width)
    d_key_low = d_keys.astype(jnp.bfloat16).reshape(-1, model_width)
    d_value_low = d_values.astype(jnp.bfloat16).reshape(-1, model_width)
    d_normed = (
        back_product(d_query_low, w_query)
        + back_product(d_key_low, w_key)
        + back_product(d_value_low, w_value)
    )
    d_w_query = outer_sum(normed, d_query_low)
    d_w_key = outer_sum(normed, d_key_low)
    d_w_value = outer_sum(normed, d_value_low)
    first_pull = jax.vjp(layer_norm, row_data, g_one, b_one)[1]
    d_rows_norm, d_g_one, d_b_one = first_pull(d_normed)
    d_rows = (d_first + d_rows_norm).astype(jnp.bfloat16).reshape(tables, local_rows, model_width)
    grads_local = (
        d_w_query,
        d_w_key,
        d_w_value,
        d_w_out,
        d_w_up,
        d_w_down,
        d_b_up,
        d_b_down,
        d_g_one,
        d_b_one,
        d_g_two,
        d_b_two,
    )
    summed = lax.psum(
        (
            grads_local[0],
            grads_local[1],
            grads_local[2],
            grads_local[3],
            grads_local[4],
            grads_local[5],
            grads_local[6],
            grads_local[7],
            grads_local[8],
            grads_local[9],
            grads_local[10],
            grads_local[11],
        ),
        ("grp", "rows"),
    )
    return (result, d_rows) + tuple(summed)


def solution(mesh):
    placed = (
        P("rows", "grp", None),
        P("rows", "grp", None),
        P(),
        P(),
        P(),
        P(),
        P(),
        P(),
        P(),
        P(),
        P(),
        P(),
        P(),
        P(),
        P("rows"),
        P("rows"),
        P("rows", None),
    )
    return jax.shard_map(
        shards,
        mesh=mesh,
        in_specs=placed,
        out_specs=(
            P("rows", "grp", None),
            P("rows", "grp", None),
            P(),
            P(),
            P(),
            P(),
            P(),
            P(),
            P(),
            P(),
            P(),
            P(),
            P(),
            P(),
        ),
        check_vma=False,
    )
```

profile of v0, /device:TPU:0, one launch (start us, length us, event | category | flops | bytes accessed | tf_op | source)
XLA Modules:
  0.0 794.6 jit_solution(12265196143458045223)
XLA Ops:
  8.7 1.5 fusion.63
  10.8 3.0 convolution_convert_fusion.3
  13.9 3.2 convolution_convert_fusion.1
  21.4 23.8 %all-gather.5.cloned.1.call-done = bf16[2048,768]{1,0:T(8,128)(2,1)} async-done(((bf16[512,768]{1,0:T(8,128)(2,1)}), bf16[2048,768]{1,0:T(8,128)(2,1)}) %all-gather.5.cloned.1.call-update) | async-done | bytes 3145744 | tf_op jit(solution)/shard_map/all_gather | solution.py:157
  45.2 3.4 fusion.130
  48.6 1.4 copy.61
  50.0 25.9 %all-gather.7.cloned.1.call-done = bf16[2048,768]{1,0:T(8,128)(2,1)} async-done(((bf16[512,768]{1,0:T(8,128)(2,1)}), bf16[2048,768]{1,0:T(8,128)(2,1)}) %all-gather.7.cloned.1.call-update) | async-done | bytes 3145744 | tf_op jit(solution)/shard_map/all_gather | solution.py:156
  75.9 3.6 fusion.129
  79.5 1.5 copy.63
  81.0 2.6 copy.58
  83.6 2.3 copy.60
  85.9 2.3 copy.55
  88.2 2.3 copy.57
  90.4 10.0 %fusion.133 = (f32[4,512]{1,0:T(4,128)}, f32[4,512,2048]{2,1,0:T(8,128)}) fusion(pred[2048]{0:T(1024)(128)(4,1)S(1)} %and_reduce_fusion, bf16[512,4,64]{0,2,1:T(8,128)(2,1)} %bitcast.194, bf16[2048,4,64]{0,2,1:T(8,128)(2,1)S(1)} %bitcast.181), kind=kOutput, calls=%fused_computation.164 | convolution fusion | flops 553650176 | bytes 18098176 | tf_op jit(solution)/shard_map/while/body/eval_jaxpr/sub | solution.py:62
  100.4 9.6 %fusion.134 = (f32[4,512]{1,0:T(4,128)S(1)}, f32[4,512,2048]{2,1,0:T(8,128)}) fusion(pred[2048]{0:T(1024)(128)(4,1)S(1)} %and_reduce_fusion, bf16[512,4,64]{0,2,1:T(8,128)(2,1)S(1)} %bitcast.192, bf16[2048,4,64]{0,2,1:T(8,128)(2,1)} %bitcast.183), kind=kOutput, calls=%fused_computation.165 | convolution fusion | flops 553650176 | bytes 18098176 | tf_op jit(solution)/shard_map/while/body/eval_jaxpr/sub | solution.py:62
  110.1 9.4 %fusion.135 = (f32[4,512]{1,0:T(4,128)S(1)}, f32[4,512,2048]{2,1,0:T(8,128)}) fusion(pred[2048]{0:T(1024)(128)(4,1)} %copy-done.61, bf16[512,4,64]{0,2,1:T(8,128)(2,1)S(1)} %bitcast.190, bf16[2048,4,64]{0,2,1:T(8,128)(2,1)S(1)} %bitcast.185), kind=kOutput, calls=%fused_computation.166 | convolution fusion | flops 553650176 | bytes 18098176 | tf_op jit(solution)/shard_map/while/body/eval_jaxpr/sub | solution.py:62
  119.5 8.9 %fusion.79 = bf16[4,64,512]{2,1,0:T(8,128)(2,1)S(1)} fusion(bf16[2048,4,64]{0,2,1:T(8,128)(2,1)} %bitcast.196, f32[4,512,2048]{2,1,0:T(8,128)} %get-tuple-element.107, f32[4,512]{1,0:T(4,128)S(1)} %copy-done.50), kind=kOutput, calls=%fused_computation.110 | convolution fusion | flops 545390592 | bytes 18096128 | tf_op jit(solution)/shard_map/while/body/eval_jaxpr/hqk,khd->qhd/dot_general | solution.py:65
  128.4 8.6 %fusion.76 = bf16[4,64,512]{2,1,0:T(8,128)(2,1)S(1)} fusion(bf16[2048,4,64]{0,2,1:T(8,128)(2,1)S(1)} %bitcast.198, f32[4,512,2048]{2,1,0:T(8,128)} %get-tuple-element.109, f32[4,512]{1,0:T(4,128)S(1)} %get-tuple-element.108), kind=kOutput, calls=%fused_computation.109 | convolution fusion | flops 545390592 | bytes 18096128 | tf_op jit(solution)/shard_map/while/body/eval_jaxpr/hqk,khd->qhd/dot_general | solution.py:65
  137.1 8.6 %fusion.73 = bf16[4,64,512]{2,1,0:T(8,128)(2,1)S(1)} fusion(bf16[2048,4,64]{0,2,1:T(8,128)(2,1)S(1)} %bitcast.200, f32[4,512,2048]{2,1,0:T(8,128)} %get-tuple-element.111, f32[4,512]{1,0:T(4,128)S(1)} %get-tuple-element.110), kind=kOutput, calls=%fused_computation.108 | convolution fusion | flops 545390592 | bytes 18096128 | tf_op jit(solution)/shard_map/while/body/eval_jaxpr/hqk,khd->qhd/dot_general | solution.py:65
  147.2 2.7 fusion.122
  150.0 9.0 %convert_reduce_fusion = (f32[3072]{0:T(1024)}, bf16[512,3072]{1,0:T(8,128)(2,1)S(1)}) fusion(f32[512,3072]{1,0:T(8,128)S(1)} %fusion.122, f32[3072]{0:T(1024)S(1)} %copy-done.66, bf16[3072,768]{1,0:T(8,128)(2,1)S(1)} %bitcast.220, bf16[1,512,768]{2,1,0:T(8,128)(2,1)S(1)} %copy-done.16, pred[512]{0:T(512)(128)(4,1)S(1)} %copy-done.58), kind=kOutput, calls=%fused_computation.39 | convolution fusion | flops 2453271552 | bytes 14967296 | tf_op jit(solution)/shard_map/dot_general | solution.py:33
  159.0 3.5 multiply_reduce_fusion.3
  166.1 1.8 copy.66
  167.9 1.8 copy.65
  170.5 13.8 %multiply_reduce_fusion = (f32[4,512]{1,0:T(4,128)}, f32[4,512,2048]{2,1,0:T(8,128)}) fusion(f32[4,512,2048]{2,1,0:T(8,128)} %get-tuple-element.107, f32[4,512]{1,0:T(4,128)} %get-tuple-element.106, bf16[512,4,64]{0,2,1:T(8,128)(2,1)} %bitcast.215, bf16[2048,4,64]{0,2,1:T(8,128)(2,1)S(1)} %bitcast.197), kind=kOutput, calls=%fused_computation.4 | convolution fusion | flops 549451776 | bytes 34881536 | tf_op jit(solution)/shard_map/while/body/eval_jaxpr/qhd,khd->hqk/dot_general | solution.py:90
  184.3 13.1 %multiply_reduce_fusion.1 = (f32[4,512]{1,0:T(4,128)S(1)}, f32[4,512,2048]{2,1,0:T(8,128)}) fusion(f32[4,512,2048]{2,1,0:T(8,128)} %get-tuple-element.109, f32[4,512]{1,0:T(4,128)S(1)} %get-tuple-element.108, bf16[512,4,64]{0,2,1:T(8,128)(2,1)S(1)} %bitcast.213, bf16[2048,4,64]{0,2,1:T(8,128)(2,1)S(1)} %bitcast.199), kind=kOutput, calls=%fused_computation.6 | convolution fusion | flops 549451776 | bytes 34881536 | tf_op jit(solution)/shard_map/while/body/eval_jaxpr/qhd,khd->hqk/dot_general | solution.py:90
  198.6 7.2 multiply_reduce_fusion.2
  205.8 11.6 %multiply_convert_fusion = bf16[4,512,2048]{2,1,0:T(8,128)(2,1)S(1)} fusion(f32[4,512,2048]{2,1,0:T(8,128)} %get-tuple-element.116, f32[4,512]{1,0:T(4,128)S(1)} %copy-done.52, f32[4,512,2048]{2,1,0:T(8,128)} %get-tuple-element.107, f32[4,512]{1,0:T(4,128)S(1)} %copy-done.51), kind=kLoop, calls=%fused_computation.3 | loop fusion | flops 16777216 | bytes 41959424 | tf_op jit(solution)/shard_map/while/body/eval_jaxpr/convert_element_type | solution.py:92
  217.5 1.6 fusion.36
  219.1 1.8 copy-done.1
  220.8 11.7 %multiply_convert_fusion.1 = bf16[4,512,2048]{2,1,0:T(8,128)(2,1)S(1)} fusion(f32[4,512,2048]{2,1,0:T(8,128)} %get-tuple-element.118, f32[4,512]{1,0:T(4,128)S(1)} %get-tuple-element.117, f32[4,512,2048]{2,1,0:T(8,128)} %get-tuple-element.109, f32[4,512]{1,0:T(4,128)S(1)} %get-tuple-element.108), kind=kLoop, calls=%fused_computation.5 | loop fusion | flops 16777216 | bytes 41959424 | tf_op jit(solution)/shard_map/while/body/eval_jaxpr/convert_element_type | solution.py:92
  232.6 1.6 fusion.35
  234.3 1.8 copy-done.2
  236.0 7.4 multiply_convert_fusion.2
  243.4 1.6 fusion.34
  245.0 1.6 copy-done.3
  246.7 1.8 pad_maximum_fusion
  249.5 7.6 fusion.43
  257.1 8.0 %fusion.40 = bf16[4,64,2048]{2,1,0:T(8,128)(2,1)S(1)} fusion(bf16[512,4,64]{0,2,1:T(8,128)(2,1)S(1)} %bitcast.214, f32[4,512,2048]{2,1,0:T(8,128)} %get-tuple-element.109, f32[4,512]{1,0:T(4,128)S(1)} %get-tuple-element.108), kind=kOutput, calls=%fused_computation.62 | convolution fusion | flops 545783808 | bytes 18096128 | tf_op jit(solution)/shard_map/while/body/eval_jaxpr/hqk,qhd->khd/dot_general | solution.py:101
  266.8 1.9 fusion.37
  268.7 1.9 pad_maximum_fusion.1
  271.8 3.1 fusion.97
  275.0 6.2 fusion.84
  281.2 6.3 fusion.83
  287.6 2.7 fusion.82
  290.4 2.5 fusion.95
  293.0 5.7 fusion.121
  298.8 6.1 fusion.98
  305.0 3.6 fusion.91
  308.6 18.0 %reduce-scatter.5.cloned.1.call-done = bf16[1,512,768]{1,2,0:T(8,128)(2,1)} async-done(((bf16[1,2048,768]{1,2,0:T(8,128)(2,1)}), bf16[1,512,768]{1,2,0:T(8,128)(2,1)}) %reduce-scatter.5.cloned.1.call-update) | async-done | bytes 786448 | tf_op jit(solution)/shard_map/reduce_scatter | solution.py:205
  326.6 3.6 fusion.88
  330.2 2.4 fusion.96
  332.6 9.1 %fusion.72 = bf16[1,512,768]{2,1,0:T(8,128)(2,1)} fusion(f32[512,768]{1,0:T(8,128)S(1)} %copy-done.10, bf16[3072,768]{1,0:T(8,128)(2,1)} %param.24, f32[768]{0:T(1024)S(1)} %copy-done.74, pred[512]{0:T(512)(128)(4,1)S(1)} %copy-done.60, f32[512,3072]{1,0:T(8,128)} %copy-done.80, f32[3072]{0:T(1024)S(1)} %copy-done.68), kind=kOutput, calls=%fused_computation.104 | convolution fusion | flops 2433220608 | bytes 13385216 | tf_op jit(solution)/shard_map/dot_general | solution.py:167
  342.9 1.8 fusion.127
  345.8 1.4 fusion.62
  347.2 42.5 %all-reduce = (f32[3072]{0:T(1024)}, f32[768]{0:T(1024)}, f32[768]{0:T(1024)}, f32[768]{0:T(1024)}, f32[768]{0:T(1024)}, /*index=5*/f32[768]{0:T(1024)}) all-reduce(f32[3072]{0:T(1024)} %get-tuple-element.122, f32[768]{0:T(1024)} %get-tuple-element.98, f32[768]{0:T(1024)} %get-tuple-element.62, ...), channel_id=1, replica_groups=mesh['grp'=4,'rows'=8] {'grp','rows'}, use_global_device_ids=true, to_apply=%region_26.27 | all-reduce | flops 6912 | bytes 55296 | tf_op jit(solution)/shard_map/psum | solution.py:237
  390.4 3.1 fusion.86
  393.5 371.4 %all-reduce.4.cloned.1.call-done = (f32[768,768]{1,0:T(8,128)}, f32[768,768]{1,0:T(8,128)}, f32[768,768]{1,0:T(8,128)}, f32[768,768]{1,0:T(8,128)}, f32[768,3072]{1,0:T(8,128)}, /*index=5*/f32[3072,768]{1,0:T(8,128)}) async-done(((f32[768,768]{1,0:T(8,128)}, f32[768,768]{1,0:T(8,128)}, f32[768,768]{1,0:T(8,128)}, f32[768,768]{1,0:T(8,128)}, f32[768,3072]{1,0:T(8,128)}, /*index=5*/f32[3072,768]{1,0:T(8,128)}), ...) | async-done | bytes 28311568 | tf_op jit(solution)/shard_map/psum | solution.py:237
  764.9 3.4 copy.75
  768.3 1.4 copy.76
  770.8 1.4 copy.77
  773.3 1.4 copy.78
  774.8 9.3 %copy.79 = f32[768,3072]{1,0:T(8,128)} copy(f32[768,3072]{1,0:T(8,128)} %get-tuple-element.130) | data formatting | bytes 18874368
  784.1 3.7 copy.80
  (243 shorter events, 21.1 us)
Async XLA Ops:
  7.2 3.5 copy-start
  7.2 38.0 %all-gather.5.cloned.1.call-start = ((), (), s32[]{:S(2)}) async-start(), calls=%async_computation.4 | async-start | bytes 3932160 | tf_op jit(solution)/shard_map/all_gather | solution.py:157
  8.6 9.3 %copy-start.39 = (f32[512]{0:T(512)}, f32[512]{0:T(512)S(1)}, u32[]{:S(2)}) copy-start(f32[512]{0:T(512)S(1)} %broadcast_multiply_fusion.1) | copy-start | bytes 6148
  10.7 7.2 copy-start.43
  13.8 4.2 copy-start.63
  13.8 62.0 %all-gather.7.cloned.1.call-start = ((), (), s32[]{:S(2)}) async-start(), calls=%async_computation.5 | async-start | bytes 3932160 | tf_op jit(solution)/shard_map/all_gather | solution.py:156
  17.1 287.9 %reduce-scatter.3.cloned.1.call-start = ((), (), s32[]{:S(2)}) async-start(), calls=%async_computation.2 | async-start | bytes 3932160 | tf_op jit(solution)/shard_map/reduce_scatter | solution.py:202
  20.0 80.5 %copy-start.23 = (bf16[512,256]{0,1:T(8,128)(2,1)}, bf16[512,256]{0,1:T(8,128)(2,1)S(1)}, u32[]{:S(2)}) copy-start(bf16[512,256]{0,1:T(8,128)(2,1)S(1)} %copy.59) | copy-start | bytes 786436
  20.1 89.9 %copy-start.21 = (bf16[512,256]{0,1:T(8,128)(2,1)}, bf16[512,256]{0,1:T(8,128)(2,1)S(1)}, u32[]{:S(2)}) copy-start(bf16[512,256]{0,1:T(8,128)(2,1)S(1)} %copy.56) | copy-start | bytes 786436
  21.4 79.0 %copy-start.61 = (pred[2048]{0:T(1024)(128)(4,1)}, pred[2048]{0:T(1024)(128)(4,1)S(1)}, u32[]{:S(2)}) copy-start(pred[2048]{0:T(1024)(128)(4,1)S(1)} %and_reduce_fusion) | copy-start | bytes 6148
  81.0 9.5 %copy-start.11 = (bf16[2048,256]{0,1:T(8,128)(2,1)}, bf16[2048,256]{0,1:T(8,128)(2,1)S(1)}, u32[]{:S(2)}) copy-start(bf16[2048,256]{0,1:T(8,128)(2,1)S(1)} %copy.63) | copy-start | bytes 3145732
  100.4 9.6 %copy-start.14 = (bf16[2048,256]{0,1:T(8,128)(2,1)S(1)}, bf16[2048,256]{0,1:T(8,128)(2,1)}, u32[]{:S(2)}) copy-start(bf16[2048,256]{0,1:T(8,128)(2,1)} %copy.57) | copy-start | bytes 3145732
  110.1 9.4 %copy-start.50 = (f32[4,512]{1,0:T(4,128)S(1)}, f32[4,512]{1,0:T(4,128)}, u32[]{:S(2)}) copy-start(f32[4,512]{1,0:T(4,128)} %get-tuple-element.106) | copy-start | bytes 24580
  119.5 8.9 %copy-start.27 = (bf16[2048,256]{0,1:T(8,128)(2,1)S(1)}, bf16[2048,256]{0,1:T(8,128)(2,1)}, u32[]{:S(2)}) copy-start(bf16[2048,256]{0,1:T(8,128)(2,1)} %copy.58) | copy-start | bytes 3145732
  128.4 17.4 %copy-start.75 = (bf16[4,64,512]{2,1,0:T(8,128)(2,1)}, bf16[4,64,512]{2,1,0:T(8,128)(2,1)S(1)}, u32[]{:S(2)}) copy-start(bf16[4,64,512]{2,1,0:T(8,128)(2,1)S(1)} %fusion.79) | copy-start | bytes 786436
  128.4 8.7 %copy-start.28 = (bf16[2048,256]{0,1:T(8,128)(2,1)S(1)}, bf16[2048,256]{0,1:T(8,128)(2,1)}, u32[]{:S(2)}) copy-start(bf16[2048,256]{0,1:T(8,128)(2,1)} %copy.55) | copy-start | bytes 3145732
  128.4 18.7 %slice-start.13 = ((s8[4718592]{0:T(1024)(128)(4,1)}), s8[4194304]{0:T(1024)(128)(4,1)S(1)}, s32[]{:S(2)}) async-start(s8[4718592]{0:T(1024)(128)(4,1)} %bitcast.217), calls=%async_computation.20 | async-start | bytes 8388608
  137.1 8.7 %copy-start.77 = (bf16[4,64,512]{2,1,0:T(8,128)(2,1)}, bf16[4,64,512]{2,1,0:T(8,128)(2,1)S(1)}, u32[]{:S(2)}) copy-start(bf16[4,64,512]{2,1,0:T(8,128)(2,1)S(1)} %fusion.76) | copy-start | bytes 786436
  137.1 8.7 %copy-start.62 = (bf16[768,768]{1,0:T(8,128)(2,1)S(1)}, bf16[768,768]{1,0:T(8,128)(2,1)}, u32[]{:S(2)}) copy-start(bf16[768,768]{1,0:T(8,128)(2,1)} %param.22) | copy-start | bytes 3538948
  137.1 10.0 %slice-start.14 = ((s8[4718592]{0:T(1024)(128)(4,1)}), s8[524288]{0:T(1024)(128)(4,1)S(1)}, s32[]{:S(2)}) async-start(s8[4718592]{0:T(1024)(128)(4,1)} %bitcast.217), calls=%async_computation.21 | async-start | bytes 1048576
  145.8 4.1 slice-start.15
  146.8 15.8 %copy-start.9 = (f32[512,768]{1,0:T(8,128)}, f32[512,768]{1,0:T(8,128)S(1)}, u32[]{:S(2)}) copy-start(f32[512,768]{1,0:T(8,128)S(1)} %get-tuple-element.113) | copy-start | bytes 4718596
  146.8 15.8 %copy-start.46 = (f32[512]{0:T(512)}, f32[512]{0:T(512)S(1)}, u32[]{:S(2)}) copy-start(f32[512]{0:T(512)S(1)} %broadcast_multiply_fusion) | copy-start | bytes 6148
  147.2 15.4 %copy-start.53 = (f32[512]{0:T(512)}, f32[512]{0:T(512)S(1)}, u32[]{:S(2)}) copy-start(f32[512]{0:T(512)S(1)} %fusion.105) | copy-start | bytes 6148
  150.0 9.0 %copy-start.80 = (f32[512,3072]{1,0:T(8,128)}, f32[512,3072]{1,0:T(8,128)S(1)}, u32[]{:S(2)}) copy-start(f32[512,3072]{1,0:T(8,128)S(1)} %fusion.122) | copy-start | bytes 18874372
  159.0 3.6 copy-start.81
  165.2 5.3 copy-start.26
  170.5 13.8 %copy-start.37 = (bf16[512,256]{0,1:T(8,128)(2,1)S(1)}, bf16[512,256]{0,1:T(8,128)(2,1)}, u32[]{:S(2)}) copy-start(bf16[512,256]{0,1:T(8,128)(2,1)} %copy.65) | copy-start | bytes 786436
  170.5 26.9 %slice-start.2 = ((s8[16777216]{0:T(1024)(128)(4,1)}), s8[4194304]{0:T(1024)(128)(4,1)S(1)}, s32[]{:S(2)}) async-start(s8[16777216]{0:T(1024)(128)(4,1)} %bitcast.175), calls=%async_computation.9 | async-start | bytes 8388608
  170.5 26.9 %slice-start.3 = ((s8[16777216]{0:T(1024)(128)(4,1)}), s8[4194304]{0:T(1024)(128)(4,1)S(1)}, s32[]{:S(2)}) async-start(s8[16777216]{0:T(1024)(128)(4,1)} %bitcast.175), calls=%async_computation.10 | async-start | bytes 8388608
  184.3 13.1 %slice-start.4 = ((s8[16777216]{0:T(1024)(128)(4,1)}), s8[4194304]{0:T(1024)(128)(4,1)S(1)}, s32[]{:S(2)}) async-start(s8[16777216]{0:T(1024)(128)(4,1)} %bitcast.175), calls=%async_computation.11 | async-start | bytes 8388608
  184.3 13.7 %slice-start.5 = ((s8[16777216]{0:T(1024)(128)(4,1)}), s8[4194304]{0:T(1024)(128)(4,1)S(1)}, s32[]{:S(2)}) async-start(s8[16777216]{0:T(1024)(128)(4,1)} %bitcast.175), calls=%async_computation.12 | async-start | bytes 8388608
  184.3 14.3 %copy-start.29 = (bf16[2048,256]{0,1:T(8,128)(2,1)S(1)}, bf16[2048,256]{0,1:T(8,128)(2,1)}, u32[]{:S(2)}) copy-start(bf16[2048,256]{0,1:T(8,128)(2,1)} %copy.55) | copy-start | bytes 3145732
  184.3 14.3 %copy-start.36 = (bf16[512,256]{0,1:T(8,128)(2,1)S(1)}, bf16[512,256]{0,1:T(8,128)(2,1)}, u32[]{:S(2)}) copy-start(bf16[512,256]{0,1:T(8,128)(2,1)} %copy.64) | copy-start | bytes 786436
  198.6 7.2 copy-start.51
  198.6 7.2 copy-start.52
  205.8 11.6 %copy-start.25 = (bf16[512,256]{0,1:T(8,128)(2,1)S(1)}, bf16[512,256]{0,1:T(8,128)(2,1)}, u32[]{:S(2)}) copy-start(bf16[512,256]{0,1:T(8,128)(2,1)} %copy.62) | copy-start | bytes 786436
  220.8 11.8 %copy-start.24 = (bf16[512,256]{0,1:T(8,128)(2,1)S(1)}, bf16[512,256]{0,1:T(8,128)(2,1)}, u32[]{:S(2)}) copy-start(bf16[512,256]{0,1:T(8,128)(2,1)} %copy-done.23) | copy-start | bytes 786436
  236.0 7.4 copy-start.22
  248.5 78.0 %reduce-scatter.5.cloned.1.call-start = ((), (), s32[]{:S(2)}) async-start(), calls=%async_computation.3 | async-start | bytes 3932160 | tf_op jit(solution)/shard_map/reduce_scatter | solution.py:205
  249.5 15.7 %slice-start.6 = ((s8[16777216]{0:T(1024)(128)(4,1)}), s8[4194304]{0:T(1024)(128)(4,1)S(1)}, s32[]{:S(2)}) async-start(s8[16777216]{0:T(1024)(128)(4,1)} %bitcast.177), calls=%async_computation.13 | async-start | bytes 8388608
  249.5 15.7 %slice-start.7 = ((s8[16777216]{0:T(1024)(128)(4,1)}), s8[4194304]{0:T(1024)(128)(4,1)S(1)}, s32[]{:S(2)}) async-start(s8[16777216]{0:T(1024)(128)(4,1)} %bitcast.177), calls=%async_computation.14 | async-start | bytes 8388608
  257.1 8.3 %slice-start.8 = ((s8[16777216]{0:T(1024)(128)(4,1)}), s8[4194304]{0:T(1024)(128)(4,1)S(1)}, s32[]{:S(2)}) async-start(s8[16777216]{0:T(1024)(128)(4,1)} %bitcast.177), calls=%async_computation.15 | async-start | bytes 8388608
  257.1 9.7 %slice-start.9 = ((s8[16777216]{0:T(1024)(128)(4,1)}), s8[4194304]{0:T(1024)(128)(4,1)S(1)}, s32[]{:S(2)}) async-start(s8[16777216]{0:T(1024)(128)(4,1)} %bitcast.177), calls=%async_computation.16 | async-start | bytes 8388608
  270.6 4.4 copy-start.12
  270.6 494.3 %all-reduce.4.cloned.1.call-start = ((), (), s32[]{:S(2)}) async-start(), calls=%async_computation.6 | async-start | bytes 56623104 | tf_op jit(solution)/shard_map/psum | solution.py:237
  275.0 6.2 copy-start.13
  275.0 12.6 %slice-start = ((s8[8388608]{0:T(1024)(128)(4,1)}), s8[4194304]{0:T(1024)(128)(4,1)S(1)}, s32[]{:S(2)}) async-start(s8[8388608]{0:T(1024)(128)(4,1)} %bitcast.173), calls=%async_computation.7 | async-start | bytes 8388608
  281.2 9.1 %copy-start.33 = (bf16[4,64,512]{2,1,0:T(8,128)(2,1)}, bf16[4,64,512]{2,1,0:T(8,128)(2,1)S(1)}, u32[]{:S(2)}) copy-start(bf16[4,64,512]{2,1,0:T(8,128)(2,1)S(1)} %fusion.84) | copy-start | bytes 786436
  281.2 6.3 slice-start.1
  281.2 6.3 copy-start.15
  287.6 5.3 copy-start.82
  290.4 8.3 %slice-start.17 = ((s8[6291456]{0:T(1024)(128)(4,1)}), s8[4194304]{0:T(1024)(128)(4,1)S(1)}, s32[]{:S(2)}) async-start(s8[6291456]{0:T(1024)(128)(4,1)} %bitcast.227), calls=%async_computation.24 | async-start | bytes 8388608
  293.0 5.8 copy-start.17
  293.0 5.8 copy-start.59
  293.0 5.8 copy-start.67
  293.0 5.8 slice-start.18
  298.8 6.2 copy-start.73
  332.6 9.1 %copy-start.64 = (bf16[768,768]{1,0:T(8,128)(2,1)S(1)}, bf16[768,768]{1,0:T(8,128)(2,1)}, u32[]{:S(2)}) copy-start(bf16[768,768]{1,0:T(8,128)(2,1)} %param.20) | copy-start | bytes 3538948
  332.6 9.1 %copy-start.65 = (bf16[1,512,768]{1,2,0:T(8,128)(2,1)S(1)}, bf16[1,512,768]{1,2,0:T(8,128)(2,1)}, u32[]{:S(2)}) copy-start(bf16[1,512,768]{1,2,0:T(8,128)(2,1)} %reduce-scatter.3.cloned.1.call-done) | copy-start | bytes 2359300
  344.7 45.8 %copy-start.7 = (f32[512,768]{1,0:T(8,128)S(1)}, f32[512,768]{1,0:T(8,128)}, u32[]{:S(2)}) copy-start(f32[512,768]{1,0:T(8,128)} %copy-done.6) | copy-start | bytes 4718596
  773.3 10.7 %slice-start.10 = ((s8[9437184]{0:T(1024)(128)(4,1)}), s8[4194304]{0:T(1024)(128)(4,1)S(1)}, s32[]{:S(2)}) async-start(s8[9437184]{0:T(1024)(128)(4,1)} %bitcast.179), calls=%async_computation.17 | async-start | bytes 8388608
  774.7 9.3 %slice-start.11 = ((s8[9437184]{0:T(1024)(128)(4,1)}), s8[4194304]{0:T(1024)(128)(4,1)S(1)}, s32[]{:S(2)}) async-start(s8[9437184]{0:T(1024)(128)(4,1)} %bitcast.179), calls=%async_computation.18 | async-start | bytes 8388608
  774.8 9.3 %slice-start.12 = ((s8[9437184]{0:T(1024)(128)(4,1)}), s8[1048576]{0:T(1024)(128)(4,1)S(1)}, s32[]{:S(2)}) async-start(s8[9437184]{0:T(1024)(128)(4,1)} %bitcast.179), calls=%async_computation.19 | async-start | bytes 2097152
  (43 other events, 99.1 us)
Sparse Core Ops, SparseCore 0:
  13.9 31.2 all-gather.4
  47.3 28.4 all-gather.6
  248.7 37.7 reduce-scatter.2
  288.8 37.7 reduce-scatter.4
  333.4 431.4 all-reduce.3
where the time goes:
time: 798 us; the launch traced here: 795 us
  waiting for transfers between devices  439 us (55%)
  matrix products  190 us (24%)
  local copies, waits for them, and re-layouts  61.2 us (8%)
  other arithmetic  45.2 us (6%)
  blocking collectives  42.5 us (5%)
  between operations  16.6 us (2%)
    psum x1, waiting for transfers between devices, shards(): lax.psum((grads_local[0], grads_local[1], grads_local[2], grads_local[3],...  371 us
    psum x1, blocking collectives, shards(): lax.psum((grads_local[0], grads_local[1], grads_local[2], grads_local[3],...  42.5 us
    unnamed x210, local copies, waits for them, and re-layouts  35.3 us
    dot_general x3, matrix products, attend_backward(): jnp.einsum('qhd,khd->hqk', grad_part, v_part, preferred_element_type=jnp....  34.1 us
    convert_element_type x3, other arithmetic, attend_backward(): d_scores = (probs_full * (d_probs - inner_sum)).astype(jnp.bfloat16)  30.7 us
    sub x3, matrix products, attend_forward(): exp_scores = jnp.exp(scores - highest)  29 us
    dot_general x3, matrix products, attend_forward(): jnp.einsum('hqk,khd->qhd', probs_low, v_part, preferred_element_type=jnp....  26.2 us
    slice x16, local copies, waits for them, and re-layouts, head_part(): matrix[:, first_head * DH:(first_head + group_size) * DH]  25.9 us
  transfers between devices with their start and end apart: 5, of which 4 were waited for; matrix products, arithmetic and copies ran while one was open for 11% of the time, Pallas kernels for 0%

commit v1 on v0

v1 whole, which is shorter than its diff:
```python
import jax
import jax.numpy as jnp
from jax import lax
from jax.sharding import PartitionSpec as P

H = 12
DH = 64
epsilon = 1e-05
BF = jnp.bfloat16
F32 = jnp.float32


def ln_parts(values):
    row_mean = jnp.mean(values, axis=-1, keepdims=True)
    centred = values - row_mean
    spread = jnp.mean(centred * centred, axis=-1, keepdims=True)
    inv = lax.rsqrt(spread + epsilon)
    return centred * inv, inv


def ln_back(cot, xhat, inv, gain):
    a = cot * gain
    mean_a = jnp.mean(a, axis=-1, keepdims=True)
    mean_ax = jnp.mean(a * xhat, axis=-1, keepdims=True)
    return inv * (a - mean_a - xhat * mean_ax)


def gelu_tanh(values):
    return jax.nn.gelu(values, approximate=True)


def dot(a, b, ca, cb):
    return lax.dot_general(a, b, (((ca,), (cb,)), ((), ())), preferred_element_type=F32)


class Wires:
    def __init__(self, mesh):
        self.ng, self.nr = mesh.shape["grp"], mesh.shape["rows"]
        self.gbits = self.ng.bit_length() - 1
        self.rbits = self.nr.bit_length() - 1

    def flip(self, value, stage):
        axis, bit = stage
        size = self.ng if axis == "grp" else self.nr
        pairs = [(i, i ^ (1 << bit)) for i in range(size)]
        return lax.ppermute(value, axis, pairs)

    def mine(self, stage):
        axis, bit = stage
        return (lax.axis_index(axis) >> bit) & 1

    def halve(self, value, stage, axis=0):
        b = self.mine(stage)
        send = lax.dynamic_index_in_dim(value, 1 - b, axis, keepdims=False).astype(BF)
        keep = lax.dynamic_index_in_dim(value, b, axis, keepdims=False)
        got = self.flip(send, stage)
        return (keep.astype(F32) + got.astype(F32)).astype(BF)

    def double(self, value, stage, axis=0):
        got = self.flip(value, stage)
        b = self.mine(stage)
        first = jnp.where(b == 0, value, got)
        second = jnp.where(b == 0, got, value)
        return jnp.stack([first, second], axis)

    def sum_all(self, value):
        core, x = ("grp", 0), [("grp", b) for b in range(1, self.gbits)]
        y, z = ("rows", 0), [("rows", b) for b in range(1, self.rbits)]
        assert len(x) == 1
        x = x[0]
        nz = len(z)
        r, c = value.shape[-2:]
        v = value.reshape((2, 2, 2, 2) + (2,) * nz + (-1, c))
        v = self.halve(v, core, 1)
        a, b = v[0], v[1]
        a, b = self.halve(a, x), self.halve(b, y)
        a, b = self.halve(a, y), self.halve(b, x)
        v = jnp.stack([a, b])
        for s in z:
            v = self.halve(v, s, 1)
        for s in z[::-1]:
            v = self.double(v, s, 1)
        a, b = v[0], v[1]
        a, b = self.double(a, y), self.double(b, x)
        a, b = self.double(a, x), self.double(b, y)
        v = jnp.stack([a, b])
        v = self.double(v, core, 1)
        return v.reshape(value.shape)


def head_part(matrix, first_head, group_size):
    return matrix[:, first_head * DH : (first_head + group_size) * DH].reshape(
        matrix.shape[0], group_size, DH
    )


def masked_scores(q_part, k_part, key_ok):
    scores = jnp.einsum("qhd,khd->hqk", q_part, k_part, preferred_element_type=F32) * DH ** (-0.5)
    return jnp.where(key_ok[None, None, :], scores, -1e30)


def attend_forward(queries, key_rows, value_rows, key_ok, group_size):
    pieces, highest_all, totals_all = ([], [], [])
    for h in range(0, H, group_size):
        q, k, v = (head_part(m, h, group_size) for m in (queries, key_rows, value_rows))
        scores = masked_scores(q, k, key_ok)
        highest = jnp.max(scores, axis=-1, keepdims=True)
        exp_scores = jnp.exp(scores - highest)
        total = jnp.sum(exp_scores, axis=-1, keepdims=True)
        probs_low = (exp_scores / total).astype(BF)
        mixed = jnp.einsum("hqk,khd->qhd", probs_low, v, preferred_element_type=F32)
        pieces.append(mixed.reshape(queries.shape[0], group_size * DH))
        highest_all.append(highest)
        totals_all.append(total)
    return jnp.concatenate(pieces, axis=1).astype(BF), highest_all, totals_all


def attend_backward(queries, key_rows, value_rows, key_ok, d_mixed, highs, totals, group_size):
    scale = DH ** (-0.5)
    qs, ks, vs = ([], [], [])
    for i, h in enumerate(range(0, H, group_size)):
        q, k, v, g = (head_part(m, h, group_size) for m in (queries, key_rows, value_rows, d_mixed))
        scores = masked_scores(q, k, key_ok)
        probs = jnp.exp(scores - highs[i]) / totals[i]
        probs_low = probs.astype(BF)
        d_probs = jnp.einsum("qhd,khd->hqk", g, v, preferred_element_type=F32)
        inner = jnp.sum(probs * d_probs, axis=-1, keepdims=True)
        d_scores = jnp.where(key_ok[None, None, :], probs * (d_probs - inner), 0.0).astype(BF)
        dq = jnp.einsum("hqk,khd->qhd", d_scores, k, preferred_element_type=F32) * scale
        dk = jnp.einsum("hqk,qhd->khd", d_scores, q, preferred_element_type=F32) * scale
        dv = jnp.einsum("hqk,qhd->khd", probs_low, g, preferred_element_type=F32)
        qs.append(dq.reshape(queries.shape[0], group_size * DH))
        ks.append(dk.reshape(key_rows.shape[0], group_size * DH))
        vs.append(dv.reshape(key_rows.shape[0], group_size * DH))
    return tuple(jnp.concatenate(m, axis=1).astype(BF) for m in (qs, ks, vs))


def solution(mesh):
    wires = Wires(mesh)

    def shards(
        table_rows, cotangent, w_query, w_key, w_value, w_out, w_up, w_down,
        b_up, b_down, g_one, b_one, g_two, b_two, ctx_count, qry_count, key_keep,
    ):
        tables, local, width = table_rows.shape
        assert tables == 1
        ng = wires.ng
        slots = key_keep.shape[1]
        ff = w_up.shape[1]
        me = lax.axis_index("grp")
        position = me * local + jnp.arange(local, dtype=jnp.int32)
        row_mask = (position < ctx_count[0] + qry_count[0])[:, None]
        order = jnp.arange(ng, dtype=jnp.int32) ^ me
        slot_of = (order[:, None] * local + jnp.arange(local, dtype=jnp.int32)[None, :]).reshape(-1)
        keep = jnp.take(key_keep[0].reshape(ng, local), order, axis=0).reshape(-1)
        key_ok = (slot_of < ctx_count[0]) & (keep == 1)

        rows_bf = table_rows[0]
        across = wires.flip(rows_bf, ("grp", 1))
        beside = wires.flip(rows_bf, ("grp", 0))
        corner = wires.flip(across, ("grp", 0))
        all_rows = jnp.concatenate([rows_bf, beside, across, corner], axis=0).astype(F32)
        row_data = rows_bf.astype(F32)
        xhat_all, inv_all = ln_parts(all_rows)
        normed_all = (xhat_all * g_one + b_one).astype(BF)
        normed = normed_all[:local]
        queries = dot(normed, w_query, 1, 0).astype(BF)
        key_rows = dot(normed_all, w_key, 1, 0).astype(BF)
        value_rows = dot(normed_all, w_value, 1, 0).astype(BF)

        mixed, highs, totals = attend_forward(queries, key_rows, value_rows, key_ok, 4)
        first_sum = row_data + dot(mixed, w_out, 1, 0)
        xhat2, inv2 = ln_parts(first_sum)
        normed_two = (xhat2 * g_two + b_two).astype(BF)
        hidden = dot(normed_two, w_up, 1, 0) + b_up
        active = gelu_tanh(hidden).astype(BF)
        second_sum = first_sum + dot(active, w_down, 1, 0) + b_down
        result = jnp.where(row_mask, second_sum, 0.0).astype(BF)

        grad_low = jnp.where(row_mask, cotangent[0], jnp.zeros((), BF))
        grad_out = grad_low.astype(F32)
        d_w_down = dot(active, grad_low, 0, 0)
        sum_down = wires.sum_all(d_w_down.astype(BF).reshape(64, ff // 64, width))
        d_b_down = jnp.sum(grad_out, axis=0)
        d_active = dot(grad_low, w_down, 1, 1)
        d_hidden = jax.vjp(gelu_tanh, hidden)[1](d_active)[0].astype(BF)
        d_b_up = jnp.sum(d_hidden, axis=0, dtype=F32)
        d_w_up = dot(normed_two, d_hidden, 0, 0)
        up_blocks = d_w_up.astype(BF).reshape(2, 4, width // 8, 8, ff // 8)
        up_blocks = up_blocks.transpose(0, 3, 1, 2, 4)
        sum_up = wires.sum_all(up_blocks.reshape(64, width // 8, ff // 8))
        d_normed_two = dot(d_hidden, w_up, 1, 1)
        d_g_two = jnp.sum(d_normed_two * xhat2, axis=0)
        d_b_two = jnp.sum(d_normed_two, axis=0)
        d_first = grad_out + ln_back(d_normed_two, xhat2, inv2, g_two)
        d_first_low = d_first.astype(BF)
        d_w_out = dot(mixed, d_first_low, 0, 0)
        d_mixed = dot(d_first_low, w_out, 1, 1).astype(BF)

        d_query, d_keys, d_values = attend_backward(
            queries, key_rows, value_rows, key_ok, d_mixed, highs, totals, 4
        )
        d_w_query = dot(normed, d_query, 0, 0)
        d_w_key = dot(normed_all, d_keys, 0, 0)
        d_w_value = dot(normed_all, d_values, 0, 0)
        cot = dot(d_keys, w_key, 1, 1) + dot(d_values, w_value, 1, 1)
        cot = jnp.concatenate([cot[:local] + dot(d_query, w_query, 1, 1), cot[local:]], axis=0)
        d_g_one = jnp.sum(cot * xhat_all, axis=0)
        d_b_one = jnp.sum(cot, axis=0)

        c4 = cot.reshape(2, 2, local, width)
        got = wires.flip(c4[:, 1].astype(BF), ("grp", 0))
        pair = c4[:, 0] + got.astype(F32)
        got = wires.flip(pair[1].astype(BF), ("grp", 1))
        d_normed = pair[0] + got.astype(F32)
        d_rows = (d_first + ln_back(d_normed, xhat_all[:local], inv_all[:local], g_one)).astype(BF)

        vec = jnp.concatenate([d_b_up, d_b_down, d_g_one, d_b_one, d_g_two, d_b_two])
        n_vec = vec.shape[0]
        vec = jnp.pad(vec, (0, 64 * 8 * width - n_vec)).astype(BF).reshape(64, 8, width)
        square = jnp.concatenate([d_w_query, d_w_key, d_w_value, d_w_out], axis=0).astype(BF)
        square = square.reshape(64, -1, width)
        tail = wires.sum_all(jnp.concatenate([square, vec], axis=1))
        per = square.shape[1]
        sums = tail[:, :per].reshape(4, width, width).astype(F32)
        flat = tail[:, per:].reshape(-1)[:n_vec].astype(F32)
        f_up, f_rest = flat[:ff], flat[ff:].reshape(5, width)
        out_up = sum_up.reshape(2, 8, 4, width // 8, ff // 8).transpose(0, 2, 3, 1, 4)
        return (
            result[None], d_rows[None],
            sums[0], sums[1], sums[2], sums[3],
            out_up.reshape(width, ff).astype(F32),
            sum_down.reshape(ff, width).astype(F32),
            f_up, f_rest[0], f_rest[1], f_rest[2], f_rest[3], f_rest[4],
        )

    rows3 = P("rows", "grp", None)
    placed = (rows3, rows3) + (P(),) * 12 + (P("rows"), P("rows"), P("rows", None))
    return jax.shard_map(
        shards, mesh=mesh, in_specs=placed, out_specs=(rows3, rows3) + (P(),) * 12, check_vma=False
    )
```

time: 798 us -> 660 us (0.83)
  waiting for transfers between devices: 439 us -> 134 us
  matrix products: 190 us -> 344 us
  starting transfers between devices: 0.38 us -> 58 us
  blocking collectives: 42.5 us -> 0 us
  between operations: 16.6 us -> 4.14 us
  other arithmetic: 45.2 us -> 54.6 us
    psum x1 -> x0, waiting for transfers between devices: 371 us -> none  [shards(): lax.psum((grads_local[0], grads_local[1], grads_local[2], grads_local[3],...]
    dot_general x33, matrix products: 161 us -> 313 us  [the longest x3 85.3 us: attend_backward(): jnp.einsum('hqk,khd->qhd', d_scores, k, preferred_element_type=F32) * scale]
    ppermute x0 -> x47, waiting for transfers between devices: none -> 134 us  [flip(): return lax.ppermute(value, axis, pairs)]
    ppermute x0 -> x47, starting transfers between devices: none -> 58 us  [flip(): return lax.ppermute(value, axis, pairs)]
    all_gather x2 -> x0, waiting for transfers between devices: 49.6 us -> none  [the longest x1 25.9 us: shards(): lax.all_gather(key_rows, 'grp', axis=1, tiled=True)]
    psum x1 -> x0, blocking collectives: 42.5 us -> none  [shards(): lax.psum((grads_local[0], grads_local[1], grads_local[2], grads_local[3],...]
    slice x16 -> x10, local copies, waits for them, and re-layouts: 25.9 us -> 4.93 us  [head_part(): matrix[:, first_head * DH:(first_head + group_size) * DH]]
    convert_element_type x0 -> x5, local copies, waits for them, and re-layouts: none -> 19.8 us  [the longest x2 13.6 us: shards(): out_up.reshape(width, ff).astype(F32)]
  transfers between devices with their start and end apart: 5 -> 47, of which waited for: 4 -> 23; matrix products, arithmetic and copies ran while one was open for 11% -> 13% of each run, Pallas kernels for 0% -> 0%
where the time goes in v1:
time: 660 us; the launch traced here: 655 us
  matrix products  344 us (52%)
  waiting for transfers between devices  134 us (20%)
  local copies, waits for them, and re-layouts  59.9 us (9%)
  starting transfers between devices  58 us (9%)
  other arithmetic  54.6 us (8%)
    ppermute x47, waiting for transfers between devices, flip(): return lax.ppermute(value, axis, pairs)  134 us
    dot_general x3, matrix products, attend_backward(): jnp.einsum('hqk,khd->qhd', d_scores, k, preferred_element_type=F32) * scale  85.3 us
    dot_general x3, matrix products, attend_backward(): jnp.einsum('hqk,qhd->khd', d_scores, q, preferred_element_type=F32) * scale  76.9 us
    dot_general x18, matrix products, dot(): lax.dot_general(a, b, (((ca,), (cb,)), ((), ())), preferred_element_type=...  76.7 us
    ppermute x47, starting transfers between devices, flip(): return lax.ppermute(value, axis, pairs)  58 us
    sub x3, matrix products, attend_forward(): exp_scores = jnp.exp(scores - highest)  30.6 us
    dot_general x3, matrix products, attend_forward(): mixed = jnp.einsum('hqk,khd->qhd', probs_low, v, preferred_element_type=F32)  26.1 us
    dot_general x3, matrix products, attend_backward(): d_probs = jnp.einsum('qhd,khd->hqk', g, v, preferred_element_type=F32)  24.5 us
  transfers between devices with their start and end apart: 47, of which 23 were waited for; matrix products, arithmetic and copies ran while one was open for 13% of the time, Pallas kernels for 0%

profile of v1, /device:TPU:0, one launch (start us, length us, event | category | flops | bytes accessed | tf_op | source)
XLA Modules:
  0.0 655.2 jit_solution(12848501231561936751)
XLA Ops:
  0.7 3.0 collective-permute-start.1
  3.7 17.7 %collective-permute-done.1 = bf16[512,768]{1,0:T(8,128)(2,1)S(1)} collective-permute-done((bf16[512,768]{1,0:T(8,128)(2,1)}, bf16[512,768]{1,0:T(8,128)(2,1)S(1)}, u32[]{:S(2)}, u32[]{:S(2)}) %collective-permute-start.1) | collective-permute-done | bytes 786464 | tf_op jit(solution)/shard_map/ppermute | solution.py:46
  32.7 3.6 fusion.29
  36.3 4.5 add_convert_fusion
  43.8 4.9 convolution_convert_fusion.2
  52.1 2.9 convolution_convert_fusion.3
  56.6 10.5 %fusion.228 = (f32[4,512]{1,0:T(4,128)}, f32[4,512,2048]{2,1,0:T(8,128)}) fusion(pred[2048]{0:T(1024)(128)(4,1)S(1)} %bitcast.474, bf16[512,4,64]{0,2,1:T(8,128)(2,1)S(1)} %bitcast.470, bf16[2048,4,64]{0,2,1:T(8,128)(2,1)} %bitcast.464), kind=kOutput, calls=%fused_computation.377 | convolution fusion | flops 553650176 | bytes 18098176 | tf_op jit(solution)/shard_map/sub | solution.py:108
  67.1 10.5 %fusion.230 = (f32[4,512]{1,0:T(4,128)}, f32[4,512,2048]{2,1,0:T(8,128)}) fusion(pred[2048]{0:T(1024)(128)(4,1)S(1)} %bitcast.475, bf16[512,4,64]{0,2,1:T(8,128)(2,1)} %bitcast.472, bf16[2048,4,64]{0,2,1:T(8,128)(2,1)} %bitcast.466), kind=kOutput, calls=%fused_computation.379 | convolution fusion | flops 553650176 | bytes 18098176 | tf_op jit(solution)/shard_map/sub | solution.py:108
  77.5 9.6 %fusion.229 = (f32[4,512]{1,0:T(4,128)S(1)}, f32[4,512,2048]{2,1,0:T(8,128)}) fusion(pred[2048]{0:T(1024)(128)(4,1)S(1)} %bitcast.476, bf16[512,4,64]{0,2,1:T(8,128)(2,1)S(1)} %bitcast.468, bf16[2048,4,64]{0,2,1:T(8,128)(2,1)} %bitcast.462), kind=kOutput, calls=%fused_computation.378 | convolution fusion | flops 553650176 | bytes 18098176 | tf_op jit(solution)/shard_map/sub | solution.py:108
  87.2 8.9 %fusion.130 = bf16[4,64,512]{2,1,0:T(8,128)(2,1)S(1)} fusion(bf16[2048,4,64]{0,2,1:T(8,128)(2,1)} %bitcast.448, f32[4,512,2048]{2,1,0:T(8,128)} %get-tuple-element.101, f32[4,512]{1,0:T(4,128)S(1)} %copy-done.71), kind=kOutput, calls=%fused_computation.162 | convolution fusion | flops 545390592 | bytes 18096128 | tf_op jit(solution)/shard_map/hqk,khd->qhd/dot_general | solution.py:111
  96.1 8.5 %fusion.124 = bf16[4,64,512]{2,1,0:T(8,128)(2,1)S(1)} fusion(bf16[2048,4,64]{0,2,1:T(8,128)(2,1)S(1)} %bitcast.450, f32[4,512,2048]{2,1,0:T(8,128)} %get-tuple-element.105, f32[4,512]{1,0:T(4,128)S(1)} %copy-done.73), kind=kOutput, calls=%fused_computation.160 | convolution fusion | flops 545390592 | bytes 18096128 | tf_op jit(solution)/shard_map/hqk,khd->qhd/dot_general | solution.py:111
  104.7 8.7 %fusion.127 = bf16[4,64,512]{2,1,0:T(8,128)(2,1)S(1)} fusion(bf16[2048,4,64]{0,2,1:T(8,128)(2,1)S(1)} %bitcast.446, f32[4,512,2048]{2,1,0:T(8,128)} %get-tuple-element.103, f32[4,512]{1,0:T(4,128)S(1)} %get-tuple-element.102), kind=kOutput, calls=%fused_computation.161 | convolution fusion | flops 545390592 | bytes 18096128 | tf_op jit(solution)/shard_map/hqk,khd->qhd/dot_general | solution.py:111
  114.7 2.7 fusion.218
  117.5 5.3 convolution_convert_fusion
  122.8 17.7 %fusion.232 = (bf16[3072]{0:T(1024)(128)(2,1)}, bf16[512,3072]{1,0:T(8,128)(2,1)S(1)}) fusion(f32[512,3072]{1,0:T(8,128)S(1)} %fusion.218, f32[3072]{0:T(1024)S(1)} %copy-done.55, bf16[3072,768]{1,0:T(8,128)(2,1)S(1)} %bitcast.486, bf16[1,512,768]{2,1,0:T(8,128)(2,1)S(1)} %copy-done.22, pred[512]{0:T(512)(128)(4,1)S(1)} %copy-done.48), kind=kOutput, calls=%fused_computation.381 | convolution fusion | flops 2450912256 | bytes 14961152 | tf_op jit(solution)/shard_map/dot_general | solution.py:33
  140.6 3.5 multiply_reduce_fusion.4
  144.1 4.8 convolution_convert_fusion.1
  152.4 8.0 %fusion.84 = bf16[4,64,2048]{2,1,0:T(8,128)(2,1)} fusion(bf16[512,4,64]{0,2,1:T(8,128)(2,1)S(1)} %bitcast.456, f32[4,512,2048]{2,1,0:T(8,128)} %get-tuple-element.105, f32[4,512]{1,0:T(4,128)S(1)} %copy-done.74), kind=kOutput, calls=%fused_computation.109 | convolution fusion | flops 545783808 | bytes 18096128 | tf_op jit(solution)/shard_map/hqk,qhd->khd/dot_general | solution.py:131
  160.4 8.1 %fusion.234 = f32[4,512,2048]{2,1,0:T(8,128)} fusion(bf16[512,4,64]{0,2,1:T(8,128)(2,1)S(1)} %bitcast.457, bf16[2048,4,64]{0,2,1:T(8,128)(2,1)S(1)} %bitcast.451), kind=kOutput, calls=%fused_computation.383 | convolution fusion | flops 536870912 | bytes 18087936 | tf_op jit(solution)/shard_map/qhd,khd->hqk/dot_general | solution.py:126
  168.6 28.6 %fusion.133 = bf16[4,64,512]{2,1,0:T(8,128)(2,1)} fusion(bf16[2048,4,64]{0,2,1:T(8,128)(2,1)S(1)} %bitcast.467, f32[4,512,2048]{2,1,0:T(8,128)} %fusion.234, pred[2048]{0:T(1024)(128)(4,1)S(1)} %bitcast.477, f32[4,512,2048]{2,1,0:T(8,128)} %get-tuple-element.105, f32[4,512]{1,0:T(4,128)S(1)} %copy-done.74), kind=kOutput, calls=%fused_computation.163 | convolution fusion | flops 566497280 | bytes 34875392 | tf_op jit(solution)/shard_map/hqk,khd->qhd/dot_general | solution.py:129
  197.1 24.6 %fusion.93 = bf16[4,64,2048]{2,1,0:T(8,128)(2,1)} fusion(bf16[512,4,64]{0,2,1:T(8,128)(2,1)S(1)} %bitcast.473, f32[4,512,2048]{2,1,0:T(8,128)} %fusion.234, pred[2048]{0:T(1024)(128)(4,1)S(1)} %bitcast.478, f32[4,512,2048]{2,1,0:T(8,128)} %get-tuple-element.105, f32[4,512]{1,0:T(4,128)S(1)} %copy-done.74), kind=kOutput, calls=%fused_computation.112 | convolution fusion | flops 567283712 | bytes 34875392 | tf_op jit(solution)/shard_map/hqk,qhd->khd/dot_general | solution.py:130
  221.9 8.0 %fusion.90 = bf16[4,64,2048]{2,1,0:T(8,128)(2,1)} fusion(bf16[512,4,64]{0,2,1:T(8,128)(2,1)S(1)} %bitcast.458, f32[4,512,2048]{2,1,0:T(8,128)} %get-tuple-element.101, f32[4,512]{1,0:T(4,128)S(1)} %copy-done.72), kind=kOutput, calls=%fused_computation.111 | convolution fusion | flops 545783808 | bytes 18096128 | tf_op jit(solution)/shard_map/hqk,qhd->khd/dot_general | solution.py:131
  229.9 8.2 %fusion.236 = f32[4,512,2048]{2,1,0:T(8,128)} fusion(bf16[512,4,64]{0,2,1:T(8,128)(2,1)S(1)} %bitcast.459, bf16[2048,4,64]{0,2,1:T(8,128)(2,1)S(1)} %bitcast.449), kind=kOutput, calls=%fused_computation.385 | convolution fusion | flops 536870912 | bytes 18087936 | tf_op jit(solution)/shard_map/qhd,khd->hqk/dot_general | solution.py:126
  238.1 28.1 %fusion.139 = bf16[4,64,512]{2,1,0:T(8,128)(2,1)} fusion(bf16[2048,4,64]{0,2,1:T(8,128)(2,1)S(1)} %bitcast.465, f32[4,512,2048]{2,1,0:T(8,128)} %fusion.236, pred[2048]{0:T(1024)(128)(4,1)S(1)} %bitcast.479, f32[4,512,2048]{2,1,0:T(8,128)} %get-tuple-element.101, f32[4,512]{1,0:T(4,128)S(1)} %copy-done.72), kind=kOutput, calls=%fused_computation.165 | convolution fusion | flops 566497280 | bytes 34875392 | tf_op jit(solution)/shard_map/hqk,khd->qhd/dot_general | solution.py:129
  266.2 28.6 %fusion.99 = bf16[4,64,2048]{2,1,0:T(8,128)(2,1)S(1)} fusion(bf16[512,4,64]{0,2,1:T(8,128)(2,1)S(1)} %bitcast.471, f32[4,512,2048]{2,1,0:T(8,128)} %fusion.236, pred[2048]{0:T(1024)(128)(4,1)S(1)} %bitcast.480, f32[4,512,2048]{2,1,0:T(8,128)} %get-tuple-element.101, f32[4,512]{1,0:T(4,128)} %get-tuple-element.100), kind=kOutput, calls=%fused_computation.114 | convolution fusion | flops 567283712 | bytes 34875392 | tf_op jit(solution)/shard_map/hqk,qhd->khd/dot_general | solution.py:130
  295.0 8.1 %fusion.87 = bf16[4,64,2048]{2,1,0:T(8,128)(2,1)} fusion(bf16[512,4,64]{0,2,1:T(8,128)(2,1)S(1)} %bitcast.460, f32[4,512,2048]{2,1,0:T(8,128)} %get-tuple-element.103, f32[4,512]{1,0:T(4,128)S(1)} %copy-done.70), kind=kOutput, calls=%fused_computation.110 | convolution fusion | flops 545783808 | bytes 18096128 | tf_op jit(solution)/shard_map/hqk,qhd->khd/dot_general | solution.py:131
  303.1 8.1 %fusion.235 = f32[4,512,2048]{2,1,0:T(8,128)} fusion(bf16[512,4,64]{0,2,1:T(8,128)(2,1)S(1)} %bitcast.461, bf16[2048,4,64]{0,2,1:T(8,128)(2,1)S(1)} %bitcast.447), kind=kOutput, calls=%fused_computation.384 | convolution fusion | flops 536870912 | bytes 18087936 | tf_op jit(solution)/shard_map/qhd,khd->hqk/dot_general | solution.py:126
  311.2 28.6 %fusion.136 = bf16[4,64,512]{2,1,0:T(8,128)(2,1)} fusion(bf16[2048,4,64]{0,2,1:T(8,128)(2,1)S(1)} %bitcast.463, f32[4,512,2048]{2,1,0:T(8,128)} %fusion.235, pred[2048]{0:T(1024)(128)(4,1)S(1)} %bitcast.481, f32[4,512,2048]{2,1,0:T(8,128)} %get-tuple-element.103, f32[4,512]{1,0:T(4,128)S(1)} %copy-done.70), kind=kOutput, calls=%fused_computation.164 | convolution fusion | flops 566497280 | bytes 34875392 | tf_op jit(solution)/shard_map/hqk,khd->qhd/dot_general | solution.py:129
  339.8 23.7 %fusion.96 = bf16[4,64,2048]{2,1,0:T(8,128)(2,1)S(1)} fusion(bf16[512,4,64]{0,2,1:T(8,128)(2,1)S(1)} %bitcast.469, f32[4,512,2048]{2,1,0:T(8,128)} %fusion.235, pred[2048]{0:T(1024)(128)(4,1)S(1)} %bitcast.482, f32[4,512,2048]{2,1,0:T(8,128)} %get-tuple-element.103, f32[4,512]{1,0:T(4,128)S(1)} %copy-done.70), kind=kOutput, calls=%fused_computation.113 | convolution fusion | flops 567283712 | bytes 34875392 | tf_op jit(solution)/shard_map/hqk,qhd->khd/dot_general | solution.py:130
  363.5 6.9 %convolution_convert_fusion.5 = bf16[768,768]{1,0:T(8,128)(2,1)} fusion(bf16[2048,768]{1,0:T(8,128)(2,1)} %copy-done.20, bf16[2048,256]{0,1:T(8,128)(2,1)} %bitcast.497, bf16[2048,256]{0,1:T(8,128)(2,1)} %bitcast.499, bf16[2048,256]{0,1:T(8,128)(2,1)} %bitcast.495), kind=kOutput, calls=%fused_computation.142 | convolution fusion | flops 2425946112 | bytes 7471104 | tf_op jit(solution)/shard_map/dot_general | solution.py:33
  370.5 2.8 fusion.114
  373.3 2.8 convolution_add_fusion
  376.2 3.1 convolution_convert_fusion.7
  388.2 6.1 multiply_reduce_fusion.3
  400.4 5.6 convolution_convert_fusion.6
  410.9 2.7 fusion.70
  415.5 3.1 fusion.56
  426.3 2.7 fusion.55
  429.3 17.4 %collective-permute-done.34 = bf16[2,2,2,48,768]{4,3,2,1,0:T(8,128)(2,1)S(1)} collective-permute-done((bf16[2,2,2,48,768]{4,3,2,1,0:T(8,128)(2,1)S(1)}, bf16[2,2,2,48,768]{4,3,2,1,0:T(8,128)(2,1)S(1)}, u32[]{:S(2)}, u32[]{:S(2)}) %collective-permute-start.34) | collective-permute-done | bytes 589856 | tf_op jit(solution)/shard_map/ppermute | solution.py:46
  450.5 8.9 %collective-permute-done.20 = bf16[2,2,2,96,384]{4,3,2,1,0:T(8,128)(2,1)S(1)} collective-permute-done((bf16[2,2,2,96,384]{4,3,2,1,0:T(8,128)(2,1)S(1)}, bf16[2,2,2,96,384]{4,3,2,1,0:T(8,128)(2,1)S(1)}, u32[]{:S(2)}, u32[]{:S(2)}) %collective-permute-start.20) | collective-permute-done | bytes 589856 | tf_op jit(solution)/shard_map/ppermute | solution.py:46
  463.2 8.1 %collective-permute-done.35 = bf16[2,2,48,768]{3,2,1,0:T(8,128)(2,1)S(1)} collective-permute-done((bf16[2,2,48,768]{3,2,1,0:T(8,128)(2,1)S(1)}, bf16[2,2,48,768]{3,2,1,0:T(8,128)(2,1)S(1)}, u32[]{:S(2)}, u32[]{:S(2)}) %collective-permute-start.35) | collective-permute-done | bytes 294944 | tf_op jit(solution)/shard_map/ppermute | solution.py:46
  472.9 7.1 %collective-permute-done.37 = bf16[2,2,48,768]{3,2,1,0:T(8,128)(2,1)S(1)} collective-permute-done((bf16[2,2,48,768]{3,2,1,0:T(8,128)(2,1)S(1)}, bf16[2,2,48,768]{3,2,1,0:T(8,128)(2,1)S(1)}, u32[]{:S(2)}, u32[]{:S(2)}) %collective-permute-start.37) | collective-permute-done | bytes 294944 | tf_op jit(solution)/shard_map/ppermute | solution.py:46
  483.6 4.9 collective-permute-done.23
  494.2 2.7 collective-permute-start.39
  498.2 3.4 collective-permute-start.25
  501.6 7.0 %collective-permute-done.39 = bf16[2,48,768]{2,1,0:T(8,128)(2,1)S(1)} collective-permute-done((bf16[2,48,768]{2,1,0:T(8,128)(2,1)S(1)}, bf16[2,48,768]{2,1,0:T(8,128)(2,1)S(1)}, u32[]{:S(2)}, u32[]{:S(2)}) %collective-permute-start.39) | collective-permute-done | bytes 147488 | tf_op jit(solution)/shard_map/ppermute | solution.py:46
  508.8 2.8 collective-permute-done.25
  512.1 6.4 collective-permute-start.10
  523.0 6.5 collective-permute-done.10
  531.3 6.4 collective-permute-done.41
  548.1 2.8 collective-permute-done.28
  552.0 3.0 collective-permute-done.12
  555.3 7.1 %collective-permute-done.13 = bf16[2,2,56,768]{3,2,1,0:T(8,128)(2,1)S(1)} collective-permute-done((bf16[2,2,56,768]{3,2,1,0:T(8,128)(2,1)S(1)}, bf16[2,2,56,768]{3,2,1,0:T(8,128)(2,1)S(1)}, u32[]{:S(2)}, u32[]{:S(2)}) %collective-permute-start.13) | collective-permute-done | bytes 344096 | tf_op jit(solution)/shard_map/ppermute | solution.py:46
  562.7 3.5 collective-permute-done.43
  570.3 8.5 %collective-permute-done.29 = bf16[2,2,2,96,384]{4,3,2,1,0:T(8,128)(2,1)S(1)} collective-permute-done((bf16[2,2,2,96,384]{4,3,2,1,0:T(8,128)(2,1)S(1)}, bf16[2,2,2,96,384]{4,3,2,1,0:T(8,128)(2,1)S(1)}, u32[]{:S(2)}, u32[]{:S(2)}) %collective-permute-start.29) | collective-permute-done | bytes 589856 | tf_op jit(solution)/shard_map/ppermute | solution.py:46
  579.5 4.5 collective-permute-done.14
  588.1 11.2 %collective-permute-done.15 = bf16[2,2,2,56,768]{4,3,2,1,0:T(8,128)(2,1)S(1)} collective-permute-done((bf16[2,2,2,56,768]{4,3,2,1,0:T(8,128)(2,1)S(1)}, bf16[2,2,2,56,768]{4,3,2,1,0:T(8,128)(2,1)S(1)}, u32[]{:S(2)}, u32[]{:S(2)}) %collective-permute-start.15) | collective-permute-done | bytes 688160 | tf_op jit(solution)/shard_map/ppermute | solution.py:46
  602.8 8.4 %fusion.113 = bf16[1,512,768]{2,1,0:T(8,128)(2,1)} fusion(f32[512,768]{1,0:T(8,128)S(1)} %copy-done.12, bf16[3072,768]{1,0:T(8,128)(2,1)S(1)} %bitcast.488, f32[768]{0:T(1024)S(1)} %copy-done.58, pred[512]{0:T(512)(128)(4,1)S(1)} %copy-done.49, f32[512,3072]{1,0:T(8,128)} %copy-done.68, f32[3072]{0:T(1024)S(1)} %copy-done.56), kind=kOutput, calls=%fused_computation.155 | convolution fusion | flops 2433220608 | bytes 13385216 | tf_op jit(solution)/shard_map/dot_general | solution.py:33
  615.3 4.4 copy.100
  619.6 9.2 %copy.101 = f32[2,4,96,8,384]{4,3,2,1,0:T(8,128)S(1)} copy(f32[2,4,96,8,384]{4,2,1,3,0:T(8,128)} %bitcast.418) | data formatting | bytes 18874368 | tf_op jit(solution)/shard_map/convert_element_type | solution.py:232
  628.9 5.9 copy.113
  637.4 4.8 copy.103
  647.5 3.6 slice_convert_fusion
  651.1 3.8 fusion.219
  (410 shorter events, 114.9 us)
Async XLA Ops:
  0.6 43.1 %copy-start = (bf16[768,768]{1,0:T(8,128)(2,1)S(1)}, bf16[768,768]{1,0:T(8,128)(2,1)}, u32[]{:S(2)}) copy-start(bf16[768,768]{1,0:T(8,128)(2,1)} %param.20) | copy-start | bytes 3538948
  0.7 32.0 %copy-start.5 = (bf16[1,512,768]{2,1,0:T(8,128)(2,1)S(1)}, bf16[1,512,768]{2,1,0:T(8,128)(2,1)}, u32[]{:S(2)}) copy-start(bf16[1,512,768]{2,1,0:T(8,128)(2,1)} %param.17) | copy-start | bytes 2359300
  0.7 35.6 %copy-start.38 = (f32[768]{0:T(1024)S(1)}, f32[768]{0:T(1024)}, u32[]{:S(2)}) copy-start(f32[768]{0:T(1024)} %param.27) | copy-start | bytes 9220
  0.7 20.8 %collective-permute-start.1 = (bf16[512,768]{1,0:T(8,128)(2,1)}, bf16[512,768]{1,0:T(8,128)(2,1)S(1)}, u32[]{:S(2)}, u32[]{:S(2)}) collective-permute-start(bf16[512,768]{1,0:T(8,128)(2,1)} %bitcast.431), channel_id=1, source_target_pairs={{0,16},{8,24},{16,0},{24,8},{1,17},{9,25},{17,1},{25,9},{2,18},{10... | collective-permute-start | bytes 2359304 | tf_op jit(solution)/shard_map/ppermute | solution.py:46
  3.7 26.8 %collective-permute-start = (bf16[512,768]{1,0:T(8,128)(2,1)}, bf16[512,768]{1,0:T(8,128)(2,1)S(1)}, u32[]{:S(2)}, u32[]{:S(2)}) collective-permute-start(bf16[512,768]{1,0:T(8,128)(2,1)} %bitcast.432), channel_id=1, source_target_pairs={{0,8},{8,0},{16,24},{24,16},{1,9},{9,1},{17,25},{25,17},{2,10},{10... | collective-permute-start | bytes 2359304 | tf_op jit(solution)/shard_map/ppermute | solution.py:46
  21.5 19.4 %copy-start.7 = (bf16[512,768]{1,0:T(8,128)(2,1)}, bf16[512,768]{1,0:T(8,128)(2,1)S(1)}, u32[]{:S(2)}) copy-start(bf16[512,768]{1,0:T(8,128)(2,1)S(1)} %collective-permute-done.1) | copy-start | bytes 2359300
  21.5 9.0 %collective-permute-start.2 = (bf16[512,768]{1,0:T(8,128)(2,1)S(1)}, bf16[512,768]{1,0:T(8,128)(2,1)}, u32[]{:S(2)}, u32[]{:S(2)}) collective-permute-start(bf16[512,768]{1,0:T(8,128)(2,1)S(1)} %collective-permute-done.1), channel_id=1, source_target_pairs={{0,8},{8,0},{16,24},{24,16},{1,9},{9,1},{17,25},{25,17},{2,10},{10... | collective-permute-start | bytes 2359304 | tf_op jit(solution)/shard_map/ppermute | solution.py:46
  43.6 13.0 %copy-start.31 = (bf16[512,256]{0,1:T(8,128)(2,1)}, bf16[512,256]{0,1:T(8,128)(2,1)S(1)}, u32[]{:S(2)}) copy-start(bf16[512,256]{0,1:T(8,128)(2,1)S(1)} %copy.86) | copy-start | bytes 786436
  43.8 33.7 %copy-start.29 = (bf16[512,256]{0,1:T(8,128)(2,1)}, bf16[512,256]{0,1:T(8,128)(2,1)S(1)}, u32[]{:S(2)}) copy-start(bf16[512,256]{0,1:T(8,128)(2,1)S(1)} %copy.85) | copy-start | bytes 786436
  56.6 48.0 %copy-start.15 = (bf16[2048,256]{0,1:T(8,128)(2,1)}, bf16[2048,256]{0,1:T(8,128)(2,1)S(1)}, u32[]{:S(2)}) copy-start(bf16[2048,256]{0,1:T(8,128)(2,1)S(1)} %get-tuple-element.40) | copy-start | bytes 3145732
  87.1 17.5 %copy-start.69 = (f32[4,512]{1,0:T(4,128)}, f32[4,512]{1,0:T(4,128)S(1)}, u32[]{:S(2)}) copy-start(f32[4,512]{1,0:T(4,128)S(1)} %get-tuple-element.102) | copy-start | bytes 24580
  114.3 34.6 %copy-start.11 = (f32[512,768]{1,0:T(8,128)}, f32[512,768]{1,0:T(8,128)S(1)}, u32[]{:S(2)}) copy-start(f32[512,768]{1,0:T(8,128)S(1)} %get-tuple-element.107) | copy-start | bytes 4718596
  168.6 28.6 %copy-start.33 = (bf16[512,256]{0,1:T(8,128)(2,1)S(1)}, bf16[512,256]{0,1:T(8,128)(2,1)}, u32[]{:S(2)}) copy-start(bf16[512,256]{0,1:T(8,128)(2,1)} %copy.84) | copy-start | bytes 786436
  197.1 24.8 %copy-start.72 = (f32[4,512]{1,0:T(4,128)S(1)}, f32[4,512]{1,0:T(4,128)}, u32[]{:S(2)}) copy-start(f32[4,512]{1,0:T(4,128)} %get-tuple-element.100) | copy-start | bytes 24580
  238.1 28.1 %copy-start.32 = (bf16[512,256]{0,1:T(8,128)(2,1)S(1)}, bf16[512,256]{0,1:T(8,128)(2,1)}, u32[]{:S(2)}) copy-start(bf16[512,256]{0,1:T(8,128)(2,1)} %copy-done.31) | copy-start | bytes 786436
  266.2 28.8 %copy-start.70 = (f32[4,512]{1,0:T(4,128)S(1)}, f32[4,512]{1,0:T(4,128)}, u32[]{:S(2)}) copy-start(f32[4,512]{1,0:T(4,128)} %copy-done.69) | copy-start | bytes 24580
  294.8 75.6 %copy-start.60 = (bf16[4,64,2048]{2,1,0:T(8,128)(2,1)}, bf16[4,64,2048]{2,1,0:T(8,128)(2,1)S(1)}, u32[]{:S(2)}) copy-start(bf16[4,64,2048]{2,1,0:T(8,128)(2,1)S(1)} %fusion.99) | copy-start | bytes 3145732
  311.2 28.6 %copy-start.30 = (bf16[512,256]{0,1:T(8,128)(2,1)S(1)}, bf16[512,256]{0,1:T(8,128)(2,1)}, u32[]{:S(2)}) copy-start(bf16[512,256]{0,1:T(8,128)(2,1)} %copy-done.29) | copy-start | bytes 786436
  387.7 27.8 %collective-permute-start.33 = (bf16[2,2,2,2,2,48,768]{6,5,4,3,2,1,0:T(8,128)(2,1)}, bf16[2,2,2,2,2,48,768]{6,5,4,3,2,1,0:T(8,128)(2,1)}, u32[]{:S(2)}, u32[]{:S(2)}) collective-permute-start(bf16[2,2,2,2,2,48,768]{6,5,4,3,2,1,0:T(8,128)(2,1)} %dynamic-slice_bitcast_fusion), channel_id=1, source_target_pairs={{0,8},{8,0},{16,24},{24,16},{1,9},{9,1},{17,25},{25,17},{2,10},{10... | collective-permute-start | bytes 7077896 | tf_op jit(solution)/shard_map/ppermute | solution.py:46
  388.1 33.2 %collective-permute-start.19 = (bf16[2,2,2,2,2,96,384]{6,5,4,3,2,1,0:T(8,128)(2,1)}, bf16[2,2,2,2,2,96,384]{6,5,4,3,2,1,0:T(8,128)(2,1)}, u32[]{:S(2)}, u32[]{:S(2)}) collective-permute-start(bf16[2,2,2,2,2,96,384]{6,5,4,3,2,1,0:T(8,128)(2,1)} %dynamic-slice_bitcast_fusion.1), channel_id=1, source_target_pairs={{0,8},{8,0},{16,24},{24,16},{1,9},{9,1},{17,25},{25,17},{2,10},{10... | collective-permute-start | bytes 7077896 | tf_op jit(solution)/shard_map/ppermute | solution.py:46
  388.2 11.4 %copy-start.45 = (bf16[768]{0:T(1024)(128)(2,1)S(1)}, bf16[768]{0:T(1024)(128)(2,1)}, u32[]{:S(2)}) copy-start(bf16[768]{0:T(1024)(128)(2,1)} %get-tuple-element.19) | copy-start | bytes 4612
  398.2 12.6 %collective-permute-start.3 = (bf16[2,512,768]{2,1,0:T(8,128)(2,1)}, bf16[2,512,768]{2,1,0:T(8,128)(2,1)}, u32[]{:S(2)}, u32[]{:S(2)}) collective-permute-start(bf16[2,512,768]{2,1,0:T(8,128)(2,1)} %fusion.108), channel_id=1, source_target_pairs={{0,8},{8,0},{16,24},{24,16},{1,9},{9,1},{17,25},{25,17},{2,10},{10... | collective-permute-start | bytes 4718600 | tf_op jit(solution)/shard_map/ppermute | solution.py:46
  410.8 14.5 %collective-permute-start.5 = (bf16[2,2,2,2,2,56,768]{6,5,4,3,2,1,0:T(8,128)(2,1)}, bf16[2,2,2,2,2,56,768]{6,5,4,3,2,1,0:T(8,128)(2,1)}, u32[]{:S(2)}, u32[]{:S(2)}) collective-permute-start(bf16[2,2,2,2,2,56,768]{6,5,4,3,2,1,0:T(8,128)(2,1)} %fusion.72), channel_id=1, source_target_pairs={{0,8},{8,0},{16,24},{24,16},{1,9},{9,1},{17,25},{25,17},{2,10},{10... | collective-permute-start | bytes 8257544 | tf_op jit(solution)/shard_map/ppermute | solution.py:46
  413.6 197.7 %collective-permute-start.4 = (bf16[512,768]{1,0:T(8,128)(2,1)S(1)}, bf16[512,768]{1,0:T(8,128)(2,1)S(1)}, u32[]{:S(2)}, u32[]{:S(2)}) collective-permute-start(bf16[512,768]{1,0:T(8,128)(2,1)S(1)} %fusion.147), channel_id=1, source_target_pairs={{0,16},{8,24},{16,0},{24,8},{1,17},{9,25},{17,1},{25,9},{2,18},{10... | collective-permute-start | bytes 2359304 | tf_op jit(solution)/shard_map/ppermute | solution.py:46
  418.8 28.0 %collective-permute-start.34 = (bf16[2,2,2,48,768]{4,3,2,1,0:T(8,128)(2,1)S(1)}, bf16[2,2,2,48,768]{4,3,2,1,0:T(8,128)(2,1)S(1)}, u32[]{:S(2)}, u32[]{:S(2)}) collective-permute-start(bf16[2,2,2,48,768]{4,3,2,1,0:T(8,128)(2,1)S(1)} %dynamic-slice_bitcast_fusion.5), channel_id=1, source_target_pairs={{0,16},{8,24},{16,0},{24,8},{1,17},{9,25},{17,1},{25,9},{2,18},{10... | collective-permute-start | bytes 1769480 | tf_op jit(solution)/shard_map/ppermute | solution.py:46
  419.4 29.3 %collective-permute-start.36 = (bf16[2,2,2,48,768]{4,3,2,1,0:T(8,128)(2,1)S(1)}, bf16[2,2,2,48,768]{4,3,2,1,0:T(8,128)(2,1)S(1)}, u32[]{:S(2)}, u32[]{:S(2)}) collective-permute-start(bf16[2,2,2,48,768]{4,3,2,1,0:T(8,128)(2,1)S(1)} %dynamic-slice_bitcast_fusion.4), channel_id=1, source_target_pairs={{0,1},{1,0},{2,3},{3,2},{4,5},{5,4},{6,7},{7,6},{8,9},{9,8},{10,11... | collective-permute-start | bytes 1769480 | tf_op jit(solution)/shard_map/ppermute | solution.py:46
  424.1 35.3 %collective-permute-start.20 = (bf16[2,2,2,96,384]{4,3,2,1,0:T(8,128)(2,1)S(1)}, bf16[2,2,2,96,384]{4,3,2,1,0:T(8,128)(2,1)S(1)}, u32[]{:S(2)}, u32[]{:S(2)}) collective-permute-start(bf16[2,2,2,96,384]{4,3,2,1,0:T(8,128)(2,1)S(1)} %dynamic-slice_bitcast_fusion.7), channel_id=1, source_target_pairs={{0,16},{8,24},{16,0},{24,8},{1,17},{9,25},{17,1},{25,9},{2,18},{10... | collective-permute-start | bytes 1769480 | tf_op jit(solution)/shard_map/ppermute | solution.py:46
  425.4 35.9 %collective-permute-start.22 = (bf16[2,2,2,96,384]{4,3,2,1,0:T(8,128)(2,1)S(1)}, bf16[2,2,2,96,384]{4,3,2,1,0:T(8,128)(2,1)S(1)}, u32[]{:S(2)}, u32[]{:S(2)}) collective-permute-start(bf16[2,2,2,96,384]{4,3,2,1,0:T(8,128)(2,1)S(1)} %dynamic-slice_bitcast_fusion.6), channel_id=1, source_target_pairs={{0,1},{1,0},{2,3},{3,2},{4,5},{5,4},{6,7},{7,6},{8,9},{9,8},{10,11... | collective-permute-start | bytes 1769480 | tf_op jit(solution)/shard_map/ppermute | solution.py:46
  446.8 43.8 %collective-permute-start.6 = (bf16[2,2,2,56,768]{4,3,2,1,0:T(8,128)(2,1)S(1)}, bf16[2,2,2,56,768]{4,3,2,1,0:T(8,128)(2,1)S(1)}, u32[]{:S(2)}, u32[]{:S(2)}) collective-permute-start(bf16[2,2,2,56,768]{4,3,2,1,0:T(8,128)(2,1)S(1)} %dynamic-slice_bitcast_fusion.3), channel_id=1, source_target_pairs={{0,16},{8,24},{16,0},{24,8},{1,17},{9,25},{17,1},{25,9},{2,18},{10... | collective-permute-start | bytes 2064392 | tf_op jit(solution)/shard_map/ppermute | solution.py:46
  448.7 43.7 %collective-permute-start.8 = (bf16[2,2,2,56,768]{4,3,2,1,0:T(8,128)(2,1)S(1)}, bf16[2,2,2,56,768]{4,3,2,1,0:T(8,128)(2,1)S(1)}, u32[]{:S(2)}, u32[]{:S(2)}) collective-permute-start(bf16[2,2,2,56,768]{4,3,2,1,0:T(8,128)(2,1)S(1)} %dynamic-slice_bitcast_fusion.2), channel_id=1, source_target_pairs={{0,1},{1,0},{2,3},{3,2},{4,5},{5,4},{6,7},{7,6},{8,9},{9,8},{10,11... | collective-permute-start | bytes 2064392 | tf_op jit(solution)/shard_map/ppermute | solution.py:46
  459.4 11.9 %collective-permute-start.35 = (bf16[2,2,48,768]{3,2,1,0:T(8,128)(2,1)S(1)}, bf16[2,2,48,768]{3,2,1,0:T(8,128)(2,1)S(1)}, u32[]{:S(2)}, u32[]{:S(2)}) collective-permute-start(bf16[2,2,48,768]{3,2,1,0:T(8,128)(2,1)S(1)} %dynamic-slice_bitcast_fusion.11), channel_id=1, source_target_pairs={{0,1},{1,0},{2,3},{3,2},{4,5},{5,4},{6,7},{7,6},{8,9},{9,8},{10,11... | collective-permute-start | bytes 884744 | tf_op jit(solution)/shard_map/ppermute | solution.py:46
  461.4 18.6 %collective-permute-start.37 = (bf16[2,2,48,768]{3,2,1,0:T(8,128)(2,1)S(1)}, bf16[2,2,48,768]{3,2,1,0:T(8,128)(2,1)S(1)}, u32[]{:S(2)}, u32[]{:S(2)}) collective-permute-start(bf16[2,2,48,768]{3,2,1,0:T(8,128)(2,1)S(1)} %dynamic-slice_bitcast_fusion.10), channel_id=1, source_target_pairs={{0,16},{8,24},{16,0},{24,8},{1,17},{9,25},{17,1},{25,9},{2,18},{10... | collective-permute-start | bytes 884744 | tf_op jit(solution)/shard_map/ppermute | solution.py:46
  471.3 10.6 %collective-permute-start.21 = (bf16[2,2,96,384]{3,2,1,0:T(8,128)(2,1)S(1)}, bf16[2,2,96,384]{3,2,1,0:T(8,128)(2,1)S(1)}, u32[]{:S(2)}, u32[]{:S(2)}) collective-permute-start(bf16[2,2,96,384]{3,2,1,0:T(8,128)(2,1)S(1)} %dynamic-slice_bitcast_fusion.13), channel_id=1, source_target_pairs={{0,1},{1,0},{2,3},{3,2},{4,5},{5,4},{6,7},{7,6},{8,9},{9,8},{10,11... | collective-permute-start | bytes 884744 | tf_op jit(solution)/shard_map/ppermute | solution.py:46
  480.0 8.5 %collective-permute-start.23 = (bf16[2,2,96,384]{3,2,1,0:T(8,128)(2,1)S(1)}, bf16[2,2,96,384]{3,2,1,0:T(8,128)(2,1)S(1)}, u32[]{:S(2)}, u32[]{:S(2)}) collective-permute-start(bf16[2,2,96,384]{3,2,1,0:T(8,128)(2,1)S(1)} %dynamic-slice_bitcast_fusion.12), channel_id=1, source_target_pairs={{0,16},{8,24},{16,0},{24,8},{1,17},{9,25},{17,1},{25,9},{2,18},{10... | collective-permute-start | bytes 884744 | tf_op jit(solution)/shard_map/ppermute | solution.py:46
  481.9 12.3 %collective-permute-start.38 = (bf16[2,2,48,768]{3,2,1,0:T(8,128)(2,1)S(1)}, bf16[2,2,48,768]{3,2,1,0:T(8,128)(2,1)S(1)}, u32[]{:S(2)}, u32[]{:S(2)}) collective-permute-start(bf16[2,2,48,768]{3,2,1,0:T(8,128)(2,1)S(1)} %fusion.180), channel_id=1, source_target_pairs={{0,2},{1,3},{2,0},{3,1},{4,6},{5,7},{6,4},{7,5},{8,10},{9,11},{10,... | collective-permute-start | bytes 884744 | tf_op jit(solution)/shard_map/ppermute | solution.py:46
  488.7 9.4 %collective-permute-start.24 = (bf16[2,2,96,384]{3,2,1,0:T(8,128)(2,1)S(1)}, bf16[2,2,96,384]{3,2,1,0:T(8,128)(2,1)S(1)}, u32[]{:S(2)}, u32[]{:S(2)}) collective-permute-start(bf16[2,2,96,384]{3,2,1,0:T(8,128)(2,1)S(1)} %fusion.184), channel_id=1, source_target_pairs={{0,2},{1,3},{2,0},{3,1},{4,6},{5,7},{6,4},{7,5},{8,10},{9,11},{10,... | collective-permute-start | bytes 884744 | tf_op jit(solution)/shard_map/ppermute | solution.py:46
  490.8 21.0 %collective-permute-start.7 = (bf16[2,2,56,768]{3,2,1,0:T(8,128)(2,1)S(1)}, bf16[2,2,56,768]{3,2,1,0:T(8,128)(2,1)S(1)}, u32[]{:S(2)}, u32[]{:S(2)}) collective-permute-start(bf16[2,2,56,768]{3,2,1,0:T(8,128)(2,1)S(1)} %dynamic-slice_bitcast_fusion.9), channel_id=1, source_target_pairs={{0,1},{1,0},{2,3},{3,2},{4,5},{5,4},{6,7},{7,6},{8,9},{9,8},{10,11... | collective-permute-start | bytes 1032200 | tf_op jit(solution)/shard_map/ppermute | solution.py:46
  492.6 19.4 %collective-permute-start.9 = (bf16[2,2,56,768]{3,2,1,0:T(8,128)(2,1)S(1)}, bf16[2,2,56,768]{3,2,1,0:T(8,128)(2,1)S(1)}, u32[]{:S(2)}, u32[]{:S(2)}) collective-permute-start(bf16[2,2,56,768]{3,2,1,0:T(8,128)(2,1)S(1)} %dynamic-slice_bitcast_fusion.8), channel_id=1, source_target_pairs={{0,16},{8,24},{16,0},{24,8},{1,17},{9,25},{17,1},{25,9},{2,18},{10... | collective-permute-start | bytes 1032200 | tf_op jit(solution)/shard_map/ppermute | solution.py:46
  494.2 14.4 %collective-permute-start.39 = (bf16[2,48,768]{2,1,0:T(8,128)(2,1)S(1)}, bf16[2,48,768]{2,1,0:T(8,128)(2,1)S(1)}, u32[]{:S(2)}, u32[]{:S(2)}) collective-permute-start(bf16[2,48,768]{2,1,0:T(8,128)(2,1)S(1)} %dynamic-slice_bitcast_fusion.15), channel_id=1, source_target_pairs={{0,4},{1,5},{2,6},{3,7},{4,0},{5,1},{6,2},{7,3},{8,12},{9,13},{10,... | collective-permute-start | bytes 442376 | tf_op jit(solution)/shard_map/ppermute | solution.py:46
  498.2 13.4 %collective-permute-start.25 = (bf16[2,96,384]{2,1,0:T(8,128)(2,1)S(1)}, bf16[2,96,384]{2,1,0:T(8,128)(2,1)S(1)}, u32[]{:S(2)}, u32[]{:S(2)}) collective-permute-start(bf16[2,96,384]{2,1,0:T(8,128)(2,1)S(1)} %dynamic-slice_bitcast_fusion.16), channel_id=1, source_target_pairs={{0,4},{1,5},{2,6},{3,7},{4,0},{5,1},{6,2},{7,3},{8,12},{9,13},{10,... | collective-permute-start | bytes 442376 | tf_op jit(solution)/shard_map/ppermute | solution.py:46
  508.7 9.8 %collective-permute-start.40 = (bf16[2,48,768]{2,1,0:T(8,128)(2,1)S(1)}, bf16[2,48,768]{2,1,0:T(8,128)(2,1)S(1)}, u32[]{:S(2)}, u32[]{:S(2)}) collective-permute-start(bf16[2,48,768]{2,1,0:T(8,128)(2,1)S(1)} %fusion.189), channel_id=1, source_target_pairs={{0,4},{1,5},{2,6},{3,7},{4,0},{5,1},{6,2},{7,3},{8,12},{9,13},{10,... | collective-permute-start | bytes 442376 | tf_op jit(solution)/shard_map/ppermute | solution.py:46
  511.6 8.9 %collective-permute-start.26 = (bf16[2,96,384]{2,1,0:T(8,128)(2,1)S(1)}, bf16[2,96,384]{2,1,0:T(8,128)(2,1)S(1)}, u32[]{:S(2)}, u32[]{:S(2)}) collective-permute-start(bf16[2,96,384]{2,1,0:T(8,128)(2,1)S(1)} %fusion.190), channel_id=1, source_target_pairs={{0,4},{1,5},{2,6},{3,7},{4,0},{5,1},{6,2},{7,3},{8,12},{9,13},{10,... | collective-permute-start | bytes 442376 | tf_op jit(solution)/shard_map/ppermute | solution.py:46
  512.1 17.4 %collective-permute-start.10 = (bf16[2,2,56,768]{3,2,0,1:T(8,128)(2,1)S(1)}, bf16[2,2,56,768]{3,2,0,1:T(8,128)(2,1)S(1)}, u32[]{:S(2)}, u32[]{:S(2)}) collective-permute-start(bf16[2,2,56,768]{3,2,0,1:T(8,128)(2,1)S(1)} %fusion.166), channel_id=1, source_target_pairs={{0,2},{1,3},{2,0},{3,1},{4,6},{5,7},{6,4},{7,5},{8,10},{9,11},{10,... | collective-permute-start | bytes 1032200 | tf_op jit(solution)/shard_map/ppermute | solution.py:46
  518.6 19.1 %collective-permute-start.41 = (bf16[2,2,48,768]{3,2,0,1:T(8,128)(2,1)S(1)}, bf16[2,2,48,768]{3,2,0,1:T(8,128)(2,1)S(1)}, u32[]{:S(2)}, u32[]{:S(2)}) collective-permute-start(bf16[2,2,48,768]{3,2,0,1:T(8,128)(2,1)S(1)} %pad_maximum_fusion.30), channel_id=1, source_target_pairs={{0,2},{1,3},{2,0},{3,1},{4,6},{5,7},{6,4},{7,5},{8,10},{9,11},{10,... | collective-permute-start | bytes 884744 | tf_op jit(solution)/shard_map/ppermute | solution.py:46
  520.6 20.2 %collective-permute-start.27 = (bf16[2,2,96,384]{3,2,0,1:T(8,128)(2,1)S(1)}, bf16[2,2,96,384]{3,2,0,1:T(8,128)(2,1)S(1)}, u32[]{:S(2)}, u32[]{:S(2)}) collective-permute-start(bf16[2,2,96,384]{3,2,0,1:T(8,128)(2,1)S(1)} %pad_maximum_fusion.29), channel_id=1, source_target_pairs={{0,2},{1,3},{2,0},{3,1},{4,6},{5,7},{6,4},{7,5},{8,10},{9,11},{10,... | collective-permute-start | bytes 884744 | tf_op jit(solution)/shard_map/ppermute | solution.py:46
  529.6 13.6 %collective-permute-start.11 = (bf16[2,56,768]{2,1,0:T(8,128)(2,1)S(1)}, bf16[2,56,768]{2,1,0:T(8,128)(2,1)S(1)}, u32[]{:S(2)}, u32[]{:S(2)}) collective-permute-start(bf16[2,56,768]{2,1,0:T(8,128)(2,1)S(1)} %dynamic-slice_bitcast_fusion.14), channel_id=1, source_target_pairs={{0,4},{1,5},{2,6},{3,7},{4,0},{5,1},{6,2},{7,3},{8,12},{9,13},{10,... | collective-permute-start | bytes 516104 | tf_op jit(solution)/shard_map/ppermute | solution.py:46
  537.8 9.0 %collective-permute-start.42 = (bf16[2,2,48,768]{3,2,1,0:T(8,128)(2,1)S(1)}, bf16[2,2,48,768]{3,2,1,0:T(8,128)(2,1)S(1)}, u32[]{:S(2)}, u32[]{:S(2)}) collective-permute-start(bf16[2,2,48,768]{3,2,1,0:T(8,128)(2,1)S(1)} %get-tuple-element.75), channel_id=1, source_target_pairs={{0,1},{1,0},{2,3},{3,2},{4,5},{5,4},{6,7},{7,6},{8,9},{9,8},{10,11... | collective-permute-start | bytes 884744 | tf_op jit(solution)/shard_map/ppermute | solution.py:46
  538.8 9.1 %collective-permute-start.44 = (bf16[2,2,48,768]{3,2,1,0:T(8,128)(2,1)S(1)}, bf16[2,2,48,768]{3,2,1,0:T(8,128)(2,1)S(1)}, u32[]{:S(2)}, u32[]{:S(2)}) collective-permute-start(bf16[2,2,48,768]{3,2,1,0:T(8,128)(2,1)S(1)} %get-tuple-element.76), channel_id=1, source_target_pairs={{0,16},{8,24},{16,0},{24,8},{1,17},{9,25},{17,1},{25,9},{2,18},{10... | collective-permute-start | bytes 884744 | tf_op jit(solution)/shard_map/ppermute | solution.py:46
  541.0 9.9 %collective-permute-start.28 = (bf16[2,2,96,384]{3,2,1,0:T(8,128)(2,1)S(1)}, bf16[2,2,96,384]{3,2,1,0:T(8,128)(2,1)S(1)}, u32[]{:S(2)}, u32[]{:S(2)}) collective-permute-start(bf16[2,2,96,384]{3,2,1,0:T(8,128)(2,1)S(1)} %get-tuple-element.83), channel_id=1, source_target_pairs={{0,1},{1,0},{2,3},{3,2},{4,5},{5,4},{6,7},{7,6},{8,9},{9,8},{10,11... | collective-permute-start | bytes 884744 | tf_op jit(solution)/shard_map/ppermute | solution.py:46
  543.3 11.8 %collective-permute-start.30 = (bf16[2,2,96,384]{3,2,1,0:T(8,128)(2,1)S(1)}, bf16[2,2,96,384]{3,2,1,0:T(8,128)(2,1)S(1)}, u32[]{:S(2)}, u32[]{:S(2)}) collective-permute-start(bf16[2,2,96,384]{3,2,1,0:T(8,128)(2,1)S(1)} %get-tuple-element.84), channel_id=1, source_target_pairs={{0,16},{8,24},{16,0},{24,8},{1,17},{9,25},{17,1},{25,9},{2,18},{10... | collective-permute-start | bytes 884744 | tf_op jit(solution)/shard_map/ppermute | solution.py:46
  546.8 8.2 %collective-permute-start.12 = (bf16[2,56,768]{2,1,0:T(8,128)(2,1)S(1)}, bf16[2,56,768]{2,1,0:T(8,128)(2,1)S(1)}, u32[]{:S(2)}, u32[]{:S(2)}) collective-permute-start(bf16[2,56,768]{2,1,0:T(8,128)(2,1)S(1)} %fusion.170), channel_id=1, source_target_pairs={{0,4},{1,5},{2,6},{3,7},{4,0},{5,1},{6,2},{7,3},{8,12},{9,13},{10,... | collective-permute-start | bytes 516104 | tf_op jit(solution)/shard_map/ppermute | solution.py:46
  547.9 18.3 %collective-permute-start.43 = (bf16[2,2,2,48,768]{4,3,2,1,0:T(8,128)(2,1)S(1)}, bf16[2,2,2,48,768]{4,3,2,1,0:T(8,128)(2,1)S(1)}, u32[]{:S(2)}, u32[]{:S(2)}) collective-permute-start(bf16[2,2,2,48,768]{4,3,2,1,0:T(8,128)(2,1)S(1)} %pad_maximum_fusion.19), channel_id=1, source_target_pairs={{0,16},{8,24},{16,0},{24,8},{1,17},{9,25},{17,1},{25,9},{2,18},{10... | collective-permute-start | bytes 1769480 | tf_op jit(solution)/shard_map/ppermute | solution.py:46
  550.9 17.1 %collective-permute-start.45 = (bf16[2,2,2,48,768]{4,3,2,1,0:T(8,128)(2,1)S(1)}, bf16[2,2,2,48,768]{4,3,2,1,0:T(8,128)(2,1)S(1)}, u32[]{:S(2)}, u32[]{:S(2)}) collective-permute-start(bf16[2,2,2,48,768]{4,3,2,1,0:T(8,128)(2,1)S(1)} %pad_maximum_fusion.20), channel_id=1, source_target_pairs={{0,1},{1,0},{2,3},{3,2},{4,5},{5,4},{6,7},{7,6},{8,9},{9,8},{10,11... | collective-permute-start | bytes 1769480 | tf_op jit(solution)/shard_map/ppermute | solution.py:46
  555.0 23.8 %collective-permute-start.29 = (bf16[2,2,2,96,384]{4,3,2,1,0:T(8,128)(2,1)S(1)}, bf16[2,2,2,96,384]{4,3,2,1,0:T(8,128)(2,1)S(1)}, u32[]{:S(2)}, u32[]{:S(2)}) collective-permute-start(bf16[2,2,2,96,384]{4,3,2,1,0:T(8,128)(2,1)S(1)} %pad_maximum_fusion.17), channel_id=1, source_target_pairs={{0,16},{8,24},{16,0},{24,8},{1,17},{9,25},{17,1},{25,9},{2,18},{10... | collective-permute-start | bytes 1769480 | tf_op jit(solution)/shard_map/ppermute | solution.py:46
  555.1 7.3 %collective-permute-start.13 = (bf16[2,2,56,768]{3,2,1,0:T(8,128)(2,1)S(1)}, bf16[2,2,56,768]{3,2,1,0:T(8,128)(2,1)S(1)}, u32[]{:S(2)}, u32[]{:S(2)}) collective-permute-start(bf16[2,2,56,768]{3,2,1,0:T(8,128)(2,1)S(1)} %pad_maximum_fusion.22), channel_id=1, source_target_pairs={{0,2},{1,3},{2,0},{3,1},{4,6},{5,7},{6,4},{7,5},{8,10},{9,11},{10,... | collective-permute-start | bytes 1032200 | tf_op jit(solution)/shard_map/ppermute | solution.py:46
  562.4 17.0 %collective-permute-start.31 = (bf16[2,2,2,96,384]{4,3,2,1,0:T(8,128)(2,1)S(1)}, bf16[2,2,2,96,384]{4,3,2,1,0:T(8,128)(2,1)S(1)}, u32[]{:S(2)}, u32[]{:S(2)}) collective-permute-start(bf16[2,2,2,96,384]{4,3,2,1,0:T(8,128)(2,1)S(1)} %pad_maximum_fusion.18), channel_id=1, source_target_pairs={{0,1},{1,0},{2,3},{3,2},{4,5},{5,4},{6,7},{7,6},{8,9},{9,8},{10,11... | collective-permute-start | bytes 1769480 | tf_op jit(solution)/shard_map/ppermute | solution.py:46
  566.2 17.9 %collective-permute-start.14 = (bf16[2,2,56,768]{3,2,1,0:T(8,128)(2,1)S(1)}, bf16[2,2,56,768]{3,2,1,0:T(8,128)(2,1)S(1)}, u32[]{:S(2)}, u32[]{:S(2)}) collective-permute-start(bf16[2,2,56,768]{3,2,1,0:T(8,128)(2,1)S(1)} %get-tuple-element.67), channel_id=1, source_target_pairs={{0,1},{1,0},{2,3},{3,2},{4,5},{5,4},{6,7},{7,6},{8,9},{9,8},{10,11... | collective-permute-start | bytes 1032200 | tf_op jit(solution)/shard_map/ppermute | solution.py:46
  568.0 17.8 %collective-permute-start.16 = (bf16[2,2,56,768]{3,2,1,0:T(8,128)(2,1)S(1)}, bf16[2,2,56,768]{3,2,1,0:T(8,128)(2,1)S(1)}, u32[]{:S(2)}, u32[]{:S(2)}) collective-permute-start(bf16[2,2,56,768]{3,2,1,0:T(8,128)(2,1)S(1)} %get-tuple-element.68), channel_id=1, source_target_pairs={{0,16},{8,24},{16,0},{24,8},{1,17},{9,25},{17,1},{25,9},{2,18},{10... | collective-permute-start | bytes 1032200 | tf_op jit(solution)/shard_map/ppermute | solution.py:46
  578.8 56.0 %collective-permute-start.46 = (bf16[2,2,2,2,2,48,768]{6,5,4,3,2,1,0:T(8,128)(2,1)}, bf16[2,2,2,2,2,48,768]{6,5,4,3,2,1,0:T(8,128)(2,1)}, u32[]{:S(2)}, u32[]{:S(2)}) collective-permute-start(bf16[2,2,2,2,2,48,768]{6,5,4,3,2,1,0:T(8,128)(2,1)} %pad_maximum_fusion.8), channel_id=1, source_target_pairs={{0,8},{8,0},{16,24},{24,16},{1,9},{9,1},{17,25},{25,17},{2,10},{10... | collective-permute-start | bytes 7077896 | tf_op jit(solution)/shard_map/ppermute | solution.py:46
  584.2 15.1 %collective-permute-start.15 = (bf16[2,2,2,56,768]{4,3,2,1,0:T(8,128)(2,1)S(1)}, bf16[2,2,2,56,768]{4,3,2,1,0:T(8,128)(2,1)S(1)}, u32[]{:S(2)}, u32[]{:S(2)}) collective-permute-start(bf16[2,2,2,56,768]{4,3,2,1,0:T(8,128)(2,1)S(1)} %pad_maximum_fusion.15), channel_id=1, source_target_pairs={{0,16},{8,24},{16,0},{24,8},{1,17},{9,25},{17,1},{25,9},{2,18},{10... | collective-permute-start | bytes 2064392 | tf_op jit(solution)/shard_map/ppermute | solution.py:46
  585.9 14.8 %collective-permute-start.17 = (bf16[2,2,2,56,768]{4,3,2,1,0:T(8,128)(2,1)S(1)}, bf16[2,2,2,56,768]{4,3,2,1,0:T(8,128)(2,1)S(1)}, u32[]{:S(2)}, u32[]{:S(2)}) collective-permute-start(bf16[2,2,2,56,768]{4,3,2,1,0:T(8,128)(2,1)S(1)} %pad_maximum_fusion.16), channel_id=1, source_target_pairs={{0,1},{1,0},{2,3},{3,2},{4,5},{5,4},{6,7},{7,6},{8,9},{9,8},{10,11... | collective-permute-start | bytes 2064392 | tf_op jit(solution)/shard_map/ppermute | solution.py:46
  587.5 15.3 %slice-start.15 = ((s8[4718592]{0:T(1024)(128)(4,1)}), s8[524288]{0:T(1024)(128)(4,1)S(1)}, s32[]{:S(2)}) async-start(s8[4718592]{0:T(1024)(128)(4,1)} %bitcast.487), calls=%async_computation.15 | async-start | bytes 1048576
  588.0 26.1 %collective-permute-start.32 = (bf16[2,2,2,2,2,96,384]{6,5,4,3,2,1,0:T(8,128)(2,1)S(1)}, bf16[2,2,2,2,2,96,384]{6,5,4,3,2,1,0:T(8,128)(2,1)S(1)}, u32[]{:S(2)}, u32[]{:S(2)}) collective-permute-start(bf16[2,2,2,2,2,96,384]{6,5,4,3,2,1,0:T(8,128)(2,1)S(1)} %pad_maximum_fusion.7), channel_id=1, source_target_pairs={{0,8},{8,0},{16,24},{24,16},{1,9},{9,1},{17,25},{25,17},{2,10},{10... | collective-permute-start | bytes 7077896 | tf_op jit(solution)/shard_map/ppermute | solution.py:46
  602.8 39.4 %collective-permute-start.18 = (bf16[2,2,2,2,2,56,768]{6,5,4,3,2,1,0:T(8,128)(2,1)}, bf16[2,2,2,2,2,56,768]{6,5,4,3,2,1,0:T(8,128)(2,1)S(1)}, u32[]{:S(2)}, u32[]{:S(2)}) collective-permute-start(bf16[2,2,2,2,2,56,768]{6,5,4,3,2,1,0:T(8,128)(2,1)} %pad_maximum_fusion.6), channel_id=1, source_target_pairs={{0,8},{8,0},{16,24},{24,16},{1,9},{9,1},{17,25},{25,17},{2,10},{10... | collective-permute-start | bytes 8257544 | tf_op jit(solution)/shard_map/ppermute | solution.py:46
  (75 other events, 400.7 us)
